TPU v7x, 128 devices: a whole 4x4x4 slice. The times are simulated.
128 devices in a mesh: leaf: 16 (over y, z), front: 8 (over x, core).
Axes of the slice: x: 4, y: 4, z: 4, core: 2. Of those that a mesh axis runs over, the one named last changes fastest.
Arguments:
- sub_rhs: float32 [393216, 128], P(('leaf', 'front')), may hold values from -6 to 6
- sub_dinv: float32 [3072, 128, 128], P(('leaf', 'front')), as said below
- sub_off: float32 [2944, 2, 128, 128], P(('leaf', 'front')), may hold values from -0.25 to 0.25
- sub_pattern: int32 [2944, 2], P(('leaf', 'front')), may hold values from 0 to 22, as said below
- sub_update: float32 [32768, 3072], P(('leaf', 'front')), may hold values from -0.0546875 to 0.0546875
- sub_map: int32 [128, 2], replicated, may hold values from 0 to 31, as said below
- front_rhs: float32 [63488, 128], P(('leaf', 'front')), may hold values from -6 to 6
- piv_inverse: float32 [63488, 2048], P(('leaf', 'front')), as said below
- upd_factor: float32 [61440, 2048], P(('leaf', 'front')), may hold values from -0.0625 to 0.0625
- front_map: int32 [30, 16], replicated, may hold values from 0 to 31, as said below
Outputs:
- sub_solution: float32 [393216, 128], P(('leaf', 'front'))
- front_solution: float32 [63488, 128], P(('leaf', 'front'))
Inputs may be any that keep to these rules, and one draw needn't show every extreme that they name: `sub_pattern`: in entry row i - 1 of a subtree (its block row i) the first index is i - 1 and every index is below i. `sub_map`: each row names 2 different blocks of a level-1 front. `front_map`: rows are ordered by level, then by front; each row names 16 different parent blocks, and the last two rows (children of the root) name only the 16 pivot blocks. `sub_dinv`: each inverse diagonal block is full. `piv_inverse`: each front's inverse pivot block is lower triangular with a unit diagonal.
All inputs are finite; a program needn't handle non-finite values.
Results may differ from a plain program's by a relative error of at most 0.0001.
Values sent between devices are 32-bit elements; how exact they have to be, the bound alone decides.
A program may use at most 128 MiB of HBM per device.

v0:
```python
import jax
import jax.numpy as jnp
from jax import lax
from jax.sharding import PartitionSpec as P

B = 128
P_SIZE = 2048
U = 2048
SB = 24
USB = 2
K = 2


def swapped(value, axis, apart):
    mask = 2**apart
    pairs = [(source, source ^ mask) for source in range(lax.axis_size(axis))]
    return lax.ppermute(value, axis, pairs)


def lookup(lookup_table, indices):
    hits = indices[:, None] == jnp.arange(lookup_table.shape[0])[None, :]
    return jnp.sum(jnp.where(hits, lookup_table[None, :], 0), axis=1)


def target(frontal_row, piv_rows, upd_rows):
    is_pivot = frontal_row < P_SIZE
    upd_part = jnp.maximum(frontal_row - P_SIZE, 0)
    divisor = max(upd_rows, 1)
    owners = jnp.where(is_pivot, frontal_row // piv_rows, upd_part // divisor)
    position = jnp.where(is_pivot, frontal_row % piv_rows, piv_rows + upd_part % divisor)
    return (owners, position)


def doubling(gathered, bit_count):
    leaf_pos = lax.axis_index("leaf")
    for which_bit in range(bit_count):
        partner_rows = swapped(gathered, "leaf", which_bit)
        upper_side = leaf_pos >> which_bit & 1 == 1
        gathered = jnp.where(
            upper_side,
            jnp.concatenate([partner_rows, gathered], 0),
            jnp.concatenate([gathered, partner_rows], 0),
        )
    return gathered


def group_gather(local_rows, bit_count):
    gathered = lax.all_gather(local_rows, "front", axis=0, tiled=True)
    return doubling(gathered, bit_count)


def per_device(
    sub_rhs,
    sub_dinv,
    sub_off,
    sub_pattern,
    sub_update,
    sub_map,
    front_rhs,
    piv_inverse,
    upd_factor,
    front_map,
):
    highest = lax.Precision.HIGHEST
    front_size = lax.axis_size("front")
    leaf_size = lax.axis_size("leaf")
    level_count = leaf_size.bit_length()
    leaf_pos = lax.axis_index("leaf")
    front_pos = lax.axis_index("front")
    num_cols = sub_rhs.shape[1]
    blocks = sub_rhs.reshape(SB, B, num_cols)
    solved = jnp.zeros((SB, B, num_cols), jnp.float32)
    solved = solved.at[0].set(
        jnp.dot(sub_dinv[0], blocks[0], precision=highest, preferred_element_type=jnp.float32)
    )

    def advance(block_id, solved):
        remain = blocks[block_id]
        for which in range(K):
            remain = remain - jnp.dot(
                sub_off[block_id - 1, which],
                solved[sub_pattern[block_id - 1, which]],
                precision=highest,
                preferred_element_type=jnp.float32,
            )
        return solved.at[block_id].set(
            jnp.dot(
                sub_dinv[block_id], remain, precision=highest, preferred_element_type=jnp.float32
            )
        )

    solved = lax.fori_loop(1, SB, advance, solved)
    flat_rows = solved.reshape(SB * B, num_cols)
    child_update = -jnp.dot(
        sub_update, flat_rows, precision=highest, preferred_element_type=jnp.float32
    )
    first_piv = P_SIZE // front_size
    first_stride = first_piv + U // front_size
    row_ids = jnp.arange(USB * B)
    map_row = lax.dynamic_index_in_dim(
        sub_map, leaf_pos * front_size + front_pos, 0, keepdims=False
    )
    parent_block = lookup(map_row, row_ids // B)
    owners, position = target(parent_block * B + row_ids % B, first_piv, U // front_size)
    buffer = (
        jnp.zeros((front_size * first_stride, num_cols), jnp.float32)
        .at[owners * first_stride + position]
        .add(child_update)
    )
    shared = lax.psum_scatter(buffer, "front", scatter_dimension=0, tiled=True)
    results = []
    piv_offset = 0
    upd_offset = 0
    map_offset = 0
    for level in range(1, level_count + 1):
        group_span = 2 ** (level - 1)
        group_size = front_size * group_span
        piv_rows = P_SIZE // group_size
        pivot_side = shared[:piv_rows] + front_rhs[piv_offset : piv_offset + piv_rows]
        piv_all = group_gather(pivot_side, level - 1)
        solution = jnp.dot(
            piv_inverse[piv_offset : piv_offset + piv_rows],
            piv_all,
            precision=highest,
            preferred_element_type=jnp.float32,
        )
        results.append(solution)
        if level < level_count:
            upd_rows = U // group_size
            update_side = shared[piv_rows:]
            solution_all = group_gather(solution, level - 1)
            update = update_side - jnp.dot(
                upd_factor[upd_offset : upd_offset + upd_rows],
                solution_all,
                precision=highest,
                preferred_element_type=jnp.float32,
            )
            parent_piv = P_SIZE // (2 * group_size)
            parent_upd = U // (2 * group_size) if level + 1 < level_count else 0
            stride = parent_piv + parent_upd
            node_index = leaf_pos >> level - 1
            map_row = lax.dynamic_index_in_dim(
                front_map, map_offset + node_index, 0, keepdims=False
            )
            my_rank = (leaf_pos & group_span - 1) * front_size + front_pos
            row_ids = my_rank * upd_rows + jnp.arange(upd_rows)
            parent_block = lookup(map_row, row_ids // B)
            owners, position = target(parent_block * B + row_ids % B, parent_piv, parent_upd)
            buffer = (
                jnp.zeros((2 * group_size * stride, num_cols), jnp.float32)
                .at[owners * stride + position]
                .add(update)
            )
            for which_bit in reversed(range(level)):
                half_rows = buffer.shape[0] // 2
                upper_side = leaf_pos >> which_bit & 1 == 1
                kept = jnp.where(upper_side, buffer[half_rows:], buffer[:half_rows])
                given = jnp.where(upper_side, buffer[:half_rows], buffer[half_rows:])
                buffer = kept + swapped(given, "leaf", which_bit)
            shared = lax.psum_scatter(buffer, "front", scatter_dimension=0, tiled=True)
            upd_offset += upd_rows
            map_offset += leaf_size >> level - 1
        piv_offset += piv_rows
    return (flat_rows, jnp.concatenate(results, 0))


def solution(mesh):
    return jax.shard_map(
        per_device,
        mesh=mesh,
        in_specs=(
            P(("leaf", "front"), None),
            P(("leaf", "front"), None, None),
            P(("leaf", "front"), None, None, None),
            P(("leaf", "front"), None),
            P(("leaf", "front"), None),
            P(),
            P(("leaf", "front"), None),
            P(("leaf", "front"), None),
            P(("leaf", "front"), None),
            P(),
        ),
        out_specs=(P(("leaf", "front"), None), P(("leaf", "front"), None)),
        check_vma=False,
    )
```

profile of v0, /device:TPU:1, one launch (start us, length us, event | category | flops | bytes accessed | tf_op | source)
XLA Modules:
  0.0 922.8 jit_solution(10828898195683964944)
XLA Ops:
  10.8 254.9 %while.21 = (s32[]{:T(128)}, f32[24,128,128]{2,1,0:T(8,128)}, f32[24,128,128]{2,1,0:T(8,128)}, f32[24,128,128]{2,1,0:T(8,128)}, f32[23,2,128,128]{3,2,1,0:T(8,12...) while((s32[]{:T(128)}, f32[24,128,128]{2,1,0:T(8,128)}, ...), condition=%wide.region_2.3_spmd, body=%wide.region_0.2_spmd.sunk | while | flops 75546648 | bytes 789780 | solution.py:92
  274.7 33.4 %reduce-scatter.8.cloned.1.call-done = f32[512,128]{0,1:T(8,128)} async-done(((f32[4096,128]{0,1:T(8,128)}), f32[512,128]{0,1:T(8,128)}) %reduce-scatter.8.cloned.1.call-update) | async-done | bytes 262160 | tf_op jit(solution)/shard_map/reduce_scatter | solution.py:110
  309.8 25.9 %all-gather.3.cloned.1.call-done = f32[2048,128]{0,1:T(8,128)} async-done(((f32[256,128]{0,1:T(8,128)}), f32[2048,128]{0,1:T(8,128)}) %all-gather.3.cloned.1.call-update) | async-done | bytes 1048592 | tf_op jit(solution)/shard_map/all_gather | solution.py:48
  340.9 22.8 %all-gather.5.cloned.1.call-done = f32[2048,128]{0,1:T(8,128)} async-done(((f32[256,128]{0,1:T(8,128)}), f32[2048,128]{0,1:T(8,128)}) %all-gather.5.cloned.1.call-update) | async-done | bytes 1048592 | tf_op jit(solution)/shard_map/all_gather | solution.py:48
  374.4 23.1 %collective-permute-done = f32[2048,128]{0,1:T(8,128)S(1)} collective-permute-done((f32[2048,128]{0,1:T(8,128)S(1)}, f32[2048,128]{0,1:T(8,128)S(1)}, u32[]{:S(2)}, u32[]{:S(2)}) %collective-permute-start) | collective-permute-done | bytes 1048608 | tf_op jit(solution)/shard_map/ppermute | solution.py:17
  398.9 29.9 %reduce-scatter.10.cloned.1.call-done = f32[256,128]{0,1:T(8,128)} async-done(((f32[2048,128]{0,1:T(8,128)}), f32[256,128]{0,1:T(8,128)}) %reduce-scatter.10.cloned.1.call-update) | async-done | bytes 131088 | tf_op jit(solution)/shard_map/reduce_scatter | solution.py:160
  429.7 16.5 %all_gather.29 = f32[1024,128]{0,1:T(8,128)S(1)} all-gather(f32[128,128]{0,1:T(8,128)S(1)} %slice_add_fusion.1), channel_id=1, replica_groups=mesh['leaf'=16,'front'=8] {'front'}, dimensions={0}, use_global_device_ids=true | all-gather | bytes 589824 | tf_op jit(solution)/shard_map/all_gather | solution.py:48
  447.4 12.0 %collective-permute-done.1 = f32[1024,128]{0,1:T(8,128)S(1)} collective-permute-done((f32[1024,128]{0,1:T(8,128)S(1)}, f32[1024,128]{0,1:T(8,128)S(1)}, u32[]{:S(2)}, u32[]{:S(2)}) %collective-permute-start.1) | collective-permute-done | bytes 524320 | tf_op jit(solution)/shard_map/ppermute | solution.py:17
  461.7 14.0 %all_gather.30 = f32[1024,128]{0,1:T(8,128)S(1)} all-gather(f32[128,128]{0,1:T(8,128)S(1)} %convolution_bitcast_fusion.5), channel_id=1, replica_groups=mesh['leaf'=16,'front'=8] {'front'}, dimensions={0}, use_global_device_ids=true | all-gather | bytes 589824 | tf_op jit(solution)/shard_map/all_gather | solution.py:48
  477.1 11.9 %collective-permute-done.2 = f32[1024,128]{0,1:T(8,128)S(1)} collective-permute-done((f32[1024,128]{0,1:T(8,128)S(1)}, f32[1024,128]{0,1:T(8,128)S(1)}, u32[]{:S(2)}, u32[]{:S(2)}) %collective-permute-start.2) | collective-permute-done | bytes 524320 | tf_op jit(solution)/shard_map/ppermute | solution.py:17
  495.9 22.4 %collective-permute-done.3 = f32[2048,128]{1,0:T(8,128)S(1)} collective-permute-done((f32[2048,128]{1,0:T(8,128)S(1)}, f32[2048,128]{1,0:T(8,128)S(1)}, u32[]{:S(2)}, u32[]{:S(2)}) %collective-permute-start.3) | collective-permute-done | bytes 1048608 | tf_op jit(solution)/shard_map/ppermute | solution.py:17
  519.9 10.3 %collective-permute-done.4 = f32[1024,128]{1,0:T(8,128)S(1)} collective-permute-done((f32[1024,128]{1,0:T(8,128)S(1)}, f32[1024,128]{1,0:T(8,128)S(1)}, u32[]{:S(2)}, u32[]{:S(2)}) %collective-permute-start.4) | collective-permute-done | bytes 524320 | tf_op jit(solution)/shard_map/ppermute | solution.py:17
  531.2 30.5 %reduce-scatter.12.cloned.1.call-done = f32[128,128]{1,0:T(8,128)} async-done(((f32[1024,128]{1,0:T(8,128)}), f32[128,128]{1,0:T(8,128)}) %reduce-scatter.12.cloned.1.call-update) | async-done | bytes 65552 | tf_op jit(solution)/shard_map/reduce_scatter | solution.py:160
  562.5 15.9 %all_gather.31 = f32[512,128]{1,0:T(8,128)S(1)} all-gather(f32[64,128]{1,0:T(8,128)S(1)} %slice_add_fusion.2), channel_id=1, replica_groups=mesh['leaf'=16,'front'=8] {'front'}, dimensions={0}, use_global_device_ids=true | all-gather | bytes 294912 | tf_op jit(solution)/shard_map/all_gather | solution.py:48
  589.1 11.0 %collective-permute-done.6 = f32[1024,128]{1,0:T(8,128)S(1)} collective-permute-done((f32[1024,128]{1,0:T(8,128)S(1)}, f32[1024,128]{1,0:T(8,128)S(1)}, u32[]{:S(2)}, u32[]{:S(2)}) %collective-permute-start.6) | collective-permute-done | bytes 524320 | tf_op jit(solution)/shard_map/ppermute | solution.py:17
  603.1 14.6 %all_gather.32 = f32[512,128]{1,0:T(8,128)S(1)} all-gather(f32[64,128]{1,0:T(8,128)S(1)} %copy.78), channel_id=1, replica_groups=mesh['leaf'=16,'front'=8] {'front'}, dimensions={0}, use_global_device_ids=true | all-gather | bytes 294912 | tf_op jit(solution)/shard_map/all_gather | solution.py:48
  628.5 10.9 %collective-permute-done.8 = f32[1024,128]{1,0:T(8,128)S(1)} collective-permute-done((f32[1024,128]{1,0:T(8,128)S(1)}, f32[1024,128]{1,0:T(8,128)S(1)}, u32[]{:S(2)}, u32[]{:S(2)}) %collective-permute-start.8) | collective-permute-done | bytes 524320 | tf_op jit(solution)/shard_map/ppermute | solution.py:17
  644.0 21.6 %collective-permute-done.9 = f32[2048,128]{1,0:T(8,128)S(1)} collective-permute-done((f32[2048,128]{1,0:T(8,128)S(1)}, f32[2048,128]{1,0:T(8,128)S(1)}, u32[]{:S(2)}, u32[]{:S(2)}) %collective-permute-start.9) | collective-permute-done | bytes 1048608 | tf_op jit(solution)/shard_map/ppermute | solution.py:17
  685.4 31.9 %reduce-scatter.16.cloned.1.call-done = f32[64,128]{1,0:T(8,128)} async-done(((f32[512,128]{1,0:T(8,128)}), f32[64,128]{1,0:T(8,128)}) %reduce-scatter.16.cloned.1.call-update) | async-done | bytes 32784 | tf_op jit(solution)/shard_map/reduce_scatter | solution.py:160
  718.2 15.8 %all_gather.33 = f32[256,128]{1,0:T(8,128)S(1)} all-gather(f32[32,128]{1,0:T(8,128)S(1)} %copy.81), channel_id=1, replica_groups=mesh['leaf'=16,'front'=8] {'front'}, dimensions={0}, use_global_device_ids=true | all-gather | bytes 147456 | tf_op jit(solution)/shard_map/all_gather | solution.py:48
  748.6 10.4 %collective-permute-done.14 = f32[1024,128]{1,0:T(8,128)S(1)} collective-permute-done((f32[1024,128]{1,0:T(8,128)S(1)}, f32[1024,128]{1,0:T(8,128)S(1)}, u32[]{:S(2)}, u32[]{:S(2)}) %collective-permute-start.14) | collective-permute-done | bytes 524320 | tf_op jit(solution)/shard_map/ppermute | solution.py:17
  761.9 15.3 %all_gather.34 = f32[256,128]{1,0:T(8,128)S(1)} all-gather(f32[32,128]{1,0:T(8,128)S(1)} %copy.84), channel_id=1, replica_groups=mesh['leaf'=16,'front'=8] {'front'}, dimensions={0}, use_global_device_ids=true | all-gather | bytes 147456 | tf_op jit(solution)/shard_map/all_gather | solution.py:48
  832.5 34.2 %reduce-scatter.14.cloned.1.call-done = f32[16,128]{1,0:T(8,128)} async-done(((f32[128,128]{1,0:T(8,128)}), f32[16,128]{1,0:T(8,128)}) %reduce-scatter.14.cloned.1.call-update) | async-done | bytes 8208 | tf_op jit(solution)/shard_map/reduce_scatter | solution.py:160
  867.4 15.8 %all_gather.35 = f32[128,128]{1,0:T(8,128)S(1)} all-gather(f32[16,128]{1,0:T(8,128)S(1)} %slice_add_fusion.3), channel_id=1, replica_groups=mesh['leaf'=16,'front'=8] {'front'}, dimensions={0}, use_global_device_ids=true | all-gather | bytes 73728 | tf_op jit(solution)/shard_map/all_gather | solution.py:48
  (288 shorter events, 371.7 us)
Async XLA Ops:
  7.2 300.9 %reduce-scatter.8.cloned.1.call-start = ((), (), s32[]{:S(2)}) async-start(), calls=%async_computation.5 | async-start | bytes 2359296 | tf_op jit(solution)/shard_map/reduce_scatter | solution.py:110
  273.7 62.0 %all-gather.3.cloned.1.call-start = ((), (), s32[]{:S(2)}) async-start(), calls=%async_computation.6 | async-start | bytes 1179648 | tf_op jit(solution)/shard_map/all_gather | solution.py:48
  309.7 54.0 %all-gather.5.cloned.1.call-start = ((), (), s32[]{:S(2)}) async-start(), calls=%async_computation.7 | async-start | bytes 1179648 | tf_op jit(solution)/shard_map/all_gather | solution.py:48
  340.5 88.3 %reduce-scatter.10.cloned.1.call-start = ((), (), s32[]{:S(2)}) async-start(), calls=%async_computation.8 | async-start | bytes 1179648 | tf_op jit(solution)/shard_map/reduce_scatter | solution.py:160
  373.0 24.5 %collective-permute-start = (f32[2048,128]{0,1:T(8,128)S(1)}, f32[2048,128]{0,1:T(8,128)S(1)}, u32[]{:S(2)}, u32[]{:S(2)}) collective-permute-start(f32[2048,128]{0,1:T(8,128)S(1)} %broadcast_select_fusion), channel_id=1, source_target_pairs={{0,8},{8,0},{16,24},{24,16},{32,40},{40,32},{48,56},{56,48},{64,72... | collective-permute-start | bytes 3145736 | tf_op jit(solution)/shard_map/ppermute | solution.py:17
  398.7 163.0 %reduce-scatter.12.cloned.1.call-start = ((), (), s32[]{:S(2)}) async-start(), calls=%async_computation.9 | async-start | bytes 589824 | tf_op jit(solution)/shard_map/reduce_scatter | solution.py:160
  446.2 13.3 %collective-permute-start.1 = (f32[1024,128]{0,1:T(8,128)S(1)}, f32[1024,128]{0,1:T(8,128)S(1)}, u32[]{:S(2)}, u32[]{:S(2)}) collective-permute-start(f32[1024,128]{0,1:T(8,128)S(1)} %all_gather.29), channel_id=1, source_target_pairs={{0,8},{8,0},{16,24},{24,16},{32,40},{40,32},{48,56},{56,48},{64,72... | collective-permute-start | bytes 1572872 | tf_op jit(solution)/shard_map/ppermute | solution.py:17
  475.7 13.3 %collective-permute-start.2 = (f32[1024,128]{0,1:T(8,128)S(1)}, f32[1024,128]{0,1:T(8,128)S(1)}, u32[]{:S(2)}, u32[]{:S(2)}) collective-permute-start(f32[1024,128]{0,1:T(8,128)S(1)} %all_gather.30), channel_id=1, source_target_pairs={{0,8},{8,0},{16,24},{24,16},{32,40},{40,32},{48,56},{56,48},{64,72... | collective-permute-start | bytes 1572872 | tf_op jit(solution)/shard_map/ppermute | solution.py:17
  493.0 25.3 %collective-permute-start.3 = (f32[2048,128]{1,0:T(8,128)S(1)}, f32[2048,128]{1,0:T(8,128)S(1)}, u32[]{:S(2)}, u32[]{:S(2)}) collective-permute-start(f32[2048,128]{1,0:T(8,128)S(1)} %slice_select_fusion.1), channel_id=1, source_target_pairs={{0,16},{8,24},{16,0},{24,8},{32,48},{40,56},{48,32},{56,40},{64,80... | collective-permute-start | bytes 3145736 | tf_op jit(solution)/shard_map/ppermute | solution.py:17
  518.6 11.7 %collective-permute-start.4 = (f32[1024,128]{1,0:T(8,128)S(1)}, f32[1024,128]{1,0:T(8,128)S(1)}, u32[]{:S(2)}, u32[]{:S(2)}) collective-permute-start(f32[1024,128]{1,0:T(8,128)S(1)} %slice_select_fusion.4), channel_id=1, source_target_pairs={{0,8},{8,0},{16,24},{24,16},{32,40},{40,32},{48,56},{56,48},{64,72... | collective-permute-start | bytes 1572872 | tf_op jit(solution)/shard_map/ppermute | solution.py:17
  531.1 186.2 %reduce-scatter.16.cloned.1.call-start = ((), (), s32[]{:S(2)}) async-start(), calls=%async_computation.11 | async-start | bytes 294912 | tf_op jit(solution)/shard_map/reduce_scatter | solution.py:160
  578.3 7.7 collective-permute-start.5
  586.1 14.0 %collective-permute-start.6 = (f32[1024,128]{1,0:T(8,128)S(1)}, f32[1024,128]{1,0:T(8,128)S(1)}, u32[]{:S(2)}, u32[]{:S(2)}) collective-permute-start(f32[1024,128]{1,0:T(8,128)S(1)} %maximum_select_fusion.14), channel_id=1, source_target_pairs={{0,16},{8,24},{16,0},{24,8},{32,48},{40,56},{48,32},{56,40},{64,80... | collective-permute-start | bytes 1572872 | tf_op jit(solution)/shard_map/ppermute | solution.py:17
  617.6 7.7 collective-permute-start.7
  625.4 14.0 %collective-permute-start.8 = (f32[1024,128]{1,0:T(8,128)S(1)}, f32[1024,128]{1,0:T(8,128)S(1)}, u32[]{:S(2)}, u32[]{:S(2)}) collective-permute-start(f32[1024,128]{1,0:T(8,128)S(1)} %maximum_select_fusion.15), channel_id=1, source_target_pairs={{0,16},{8,24},{16,0},{24,8},{32,48},{40,56},{48,32},{56,40},{64,80... | collective-permute-start | bytes 1572872 | tf_op jit(solution)/shard_map/ppermute | solution.py:17
  642.7 22.9 %collective-permute-start.9 = (f32[2048,128]{1,0:T(8,128)S(1)}, f32[2048,128]{1,0:T(8,128)S(1)}, u32[]{:S(2)}, u32[]{:S(2)}) collective-permute-start(f32[2048,128]{1,0:T(8,128)S(1)} %slice_select_fusion), channel_id=1, source_target_pairs={{0,32},{8,40},{16,48},{24,56},{32,0},{40,8},{48,16},{56,24},{64,96... | collective-permute-start | bytes 3145736 | tf_op jit(solution)/shard_map/ppermute | solution.py:17
  665.9 12.6 %collective-permute-start.10 = (f32[1024,128]{1,0:T(8,128)S(1)}, f32[1024,128]{1,0:T(8,128)S(1)}, u32[]{:S(2)}, u32[]{:S(2)}) collective-permute-start(f32[1024,128]{1,0:T(8,128)S(1)} %slice_select_fusion.3), channel_id=1, source_target_pairs={{0,16},{8,24},{16,0},{24,8},{32,48},{40,56},{48,32},{56,40},{64,80... | collective-permute-start | bytes 1572872 | tf_op jit(solution)/shard_map/ppermute | solution.py:17
  685.2 181.4 %reduce-scatter.14.cloned.1.call-start = ((), (), s32[]{:S(2)}) async-start(), calls=%async_computation.10 | async-start | bytes 73728 | tf_op jit(solution)/shard_map/reduce_scatter | solution.py:160
  738.9 8.4 collective-permute-start.13
  747.4 11.7 %collective-permute-start.14 = (f32[1024,128]{1,0:T(8,128)S(1)}, f32[1024,128]{1,0:T(8,128)S(1)}, u32[]{:S(2)}, u32[]{:S(2)}) collective-permute-start(f32[1024,128]{1,0:T(8,128)S(1)} %maximum_select_fusion.16), channel_id=1, source_target_pairs={{0,32},{8,40},{16,48},{24,56},{32,0},{40,8},{48,16},{56,24},{64,96... | collective-permute-start | bytes 1572872 | tf_op jit(solution)/shard_map/ppermute | solution.py:17
  782.1 8.4 collective-permute-start.16
  790.6 11.7 %collective-permute-start.17 = (f32[1024,128]{1,0:T(8,128)S(1)}, f32[1024,128]{1,0:T(8,128)S(1)}, u32[]{:S(2)}, u32[]{:S(2)}) collective-permute-start(f32[1024,128]{1,0:T(8,128)S(1)} %maximum_select_fusion.17), channel_id=1, source_target_pairs={{0,32},{8,40},{16,48},{24,56},{32,0},{40,8},{48,16},{56,24},{64,96... | collective-permute-start | bytes 1572872 | tf_op jit(solution)/shard_map/ppermute | solution.py:17
  805.0 12.3 %collective-permute-start.18 = (f32[1024,128]{1,0:T(8,128)S(1)}, f32[1024,128]{1,0:T(8,128)S(1)}, u32[]{:S(2)}, u32[]{:S(2)}) collective-permute-start(f32[1024,128]{1,0:T(8,128)S(1)} %slice_select_fusion.2), channel_id=1, source_target_pairs={{0,64},{8,72},{16,80},{24,88},{32,96},{40,104},{48,112},{56,120},{... | collective-permute-start | bytes 1572872 | tf_op jit(solution)/shard_map/ppermute | solution.py:17
  897.9 12.8 %collective-permute-start.25 = (f32[1024,128]{1,0:T(8,128)S(1)}, f32[1024,128]{1,0:T(8,128)S(1)}, u32[]{:S(2)}, u32[]{:S(2)}) collective-permute-start(f32[1024,128]{1,0:T(8,128)S(1)} %maximum_select_fusion.18), channel_id=1, source_target_pairs={{0,64},{8,72},{16,80},{24,88},{32,96},{40,104},{48,112},{56,120},{... | collective-permute-start | bytes 1572872 | tf_op jit(solution)/shard_map/ppermute | solution.py:17
  (24 other events, 872.5 us)
Sparse Core Ops, SparseCore 0:
  273.8 34.2 reduce-scatter.7
  310.3 25.2 all-gather.2
  340.6 23.0 all-gather.4
  398.8 29.9 reduce-scatter.9
  531.2 30.3 reduce-scatter.11
  685.4 31.8 reduce-scatter.15
  832.6 34.0 reduce-scatter.13
where the time goes:
time: 931 us; the launch traced here: 923 us
  waiting for transfers between devices  435 us (47%)
  matrix products  136 us (15%)
  blocking collectives  108 us (12%)
  loops' own time  86.4 us (9%)
  starting transfers between devices  50.6 us (5%)
  other arithmetic  48.7 us (5%)
  local copies, waits for them, and re-layouts  44.1 us (5%)
  between operations  14.7 us (2%)
    ppermute x26, waiting for transfers between devices, swapped(): return lax.ppermute(value, axis, pairs)  226 us
    reduce_scatter x5, waiting for transfers between devices, per_device(): shared = lax.psum_scatter(buffer, 'front', scatter_dimension=0, tiled=True)  160 us
    all_gather x7, blocking collectives, group_gather(): gathered = lax.all_gather(local_rows, 'front', axis=0, tiled=True)  108 us
    another operation x1, loops' own time, per_device(): solved = lax.fori_loop(1, SB, advance, solved)  86.4 us
    dot_general x23, matrix products, advance(): jnp.dot(sub_dinv[block_id], remain, precision=highest, preferred_element_...  54.1 us
    dot_general x46, matrix products, advance(): jnp.dot(sub_off[block_id - 1, which], solved[sub_pattern[block_id - 1, wh...  50.4 us
    ppermute x26, starting transfers between devices, swapped(): return lax.ppermute(value, axis, pairs)  50.3 us
    all_gather x2, waiting for transfers between devices, group_gather(): gathered = lax.all_gather(local_rows, 'front', axis=0, tiled=True)  48.7 us
  transfers between devices with their start and end apart: 33, of which 33 were waited for; matrix products, arithmetic and copies ran while one was open for 0% of the time, Pallas kernels for 0%

commit v1 on v0

v1 whole, which is shorter than its diff:
```python
import jax
import jax.numpy as jnp
from jax import lax
from jax.experimental import pallas as pl
from jax.experimental.pallas import tpu as pltpu
from jax.sharding import PartitionSpec as P

B = 128
N = 128
SB = 24
K = 2
ROWS = 2048
PB = 16
LEVELS = 5
PROWS = 496
UROWS = 480
MAPROWS = 30
YS = (1, 1, 1, 2, 4)
ZS = (1, 2, 4, 4, 4)
HELD = (256, 128, 64, 32, 16)
MAP_AT = (0, 16, 24, 28)
ENTRY_AT = (None, 0, 18, 35, 52, 69)
ORDER = ("xzy", "yzx")
DIM_AT = {"x": 0, "z": 3, "y": 6}
COPIES = 19
F32 = jnp.float32
BF16 = jnp.bfloat16


def split(value):
    high = value.astype(BF16)
    return high, (value - high.astype(F32)).astype(BF16)


def side(value):
    return jnp.concatenate(split(value), axis=1)


def stack(value):
    return jnp.concatenate(split(value), axis=0)


def dot(left, right):
    return jnp.dot(left, right, preferred_element_type=F32)


def fold(product):
    half = product.shape[0] // 2
    return product[:half, :N] + (product[:half, N:] + product[half:, :N])


class Gather:
    def __init__(self, buf, send, recv, level, at):
        self.buf, self.send, self.recv, self.at = buf, send, recv, at
        self.size = {"x": 4, "z": ZS[level - 1], "y": YS[level - 1]}
        self.own = {
            d: 0 if self.size[d] == 1 else at[d] % self.size[d] for d in "yzx"
        }

    def dims(self, core):
        return [d for d in ORDER[core] if self.size[d] > 1]

    def view(self, full, own, core):
        index = [slice(None) if d in full else own[d] for d in "yzx"]
        return self.buf.at[index[0], index[1], index[2], core]

    def offsets(self, dim):
        return (2, 1, 3) if self.size[dim] == 4 else (1,)

    def moved(self, dim, offset):
        here = self.at[dim]
        if self.size[dim] == 4:
            return (here + offset) % 4
        return here + 1 - 2 * (here % 2)

    def copy(self, view, which, **changes):
        place = {**self.at, **changes}
        return pltpu.make_async_remote_copy(
            src_ref=view,
            dst_ref=view,
            send_sem=self.send.at[which],
            recv_sem=self.recv.at[which],
            device_id=(place["y"] * 4 + place["z"], place["x"] * 2 + place["core"]),
            device_id_type=pl.DeviceIdType.MESH,
        )

    def outgoing(self, phase, core):
        dims = self.dims(core)
        dim = dims[phase]
        view = self.view(dims[:phase], self.own, core)
        return [
            self.copy(view, DIM_AT[dim] + offset - 1, core=core, **{dim: self.moved(dim, offset)})
            for offset in self.offsets(dim)
        ]

    def incoming(self, phase, core):
        dims = self.dims(core)
        dim = dims[phase]
        found = []
        for offset in self.offsets(dim):
            origin = self.moved(dim, 4 - offset) % self.size[dim]
            view = self.view(dims[:phase], {**self.own, dim: origin}, core)
            found.append((view, DIM_AT[dim] + offset - 1))
        return found

    def shared(self, core):
        views = [self.view((), self.own, core)]
        for phase in range(len(self.dims(core))):
            views += [view for view, _ in self.incoming(phase, core)]
        return views

    def crossing(self, core, to, first=0, many=COPIES):
        views = list(enumerate(self.shared(core)))[first : first + many]
        return [self.copy(view, 9 + which, core=to) for which, view in views]

    def start(self, core):
        for copy in self.outgoing(0, core):
            copy.start()
        for copy in self.crossing(core, 1 - core, 0, 1):
            copy.start()

    def phases(self, core):
        return len(self.dims(core))

    def advance(self, phase, core):
        if phase >= self.phases(core):
            return
        first = 1 + sum(len(self.incoming(p, core)) for p in range(phase))
        arrivals = self.incoming(phase, core)
        for view, which in arrivals:
            self.copy(view, which, core=1 - core).wait_recv()
        if phase + 1 < self.phases(core):
            for copy in self.outgoing(phase + 1, core):
                copy.start()
        for copy in self.crossing(core, 1 - core, first, len(arrivals)):
            copy.start()

    def finish(self, core):
        for copy in self.crossing(1 - core, 1 - core):
            copy.wait_recv()

    def drain(self, core):
        for phase in range(self.phases(core)):
            for copy in self.outgoing(phase, core):
                copy.wait_send()
        for copy in self.crossing(core, 1 - core):
            copy.wait_send()


def kernel(
    pattern, spots, hits,
    rhs, dinv, off, update, front_rhs, piv, factor,
    solved_out, front_out,
    b_v, d_v, l_v, u_v, m_v, e_v, y_v, yhl_v, g_v, c_v, acc_v, p_v, last_v,
    h1, h2, h3, h4, h5, w0, w1, w2, w3, w4, z1, z2, z3, z4,
    load_sem, store_sem, send, recv,
):
    leaf = lax.axis_index("leaf")
    front = lax.axis_index("front")
    core = front % 2
    at = {"y": leaf // 4, "z": leaf % 4, "x": front // 2, "core": core}

    def both(step):
        for which in (0, 1):
            @pl.when(core == which)
            def _():
                step(which)

    bufs = (h1, h2, h3, h4, h5, w0, w1, w2, w3, w4, z1, z2, z3, z4)
    groups = (1, 2, 3, 4, 5, 1, 2, 3, 4, 5, 1, 2, 3, 4)
    gathers = [
        Gather(buf, send.at[g], recv.at[g], level, at)
        for g, (buf, level) in enumerate(zip(bufs, groups))
    ]
    hs, ws, zs = gathers[:5], gathers[5:10], gathers[10:]

    def mine(gather):
        own = gather.own
        return (own["y"], own["z"], own["x"], core)

    loads = []

    def load(source, target):
        copy = pltpu.make_async_copy(source, target, load_sem.at[len(loads)])
        copy.start()
        loads.append(copy)

    load(dinv, d_v)
    load(off, l_v)
    load(rhs, b_v)
    row = 0
    for gather, held in zip(hs, HELD):
        load(front_rhs.at[pl.ds(row, held)], gather.buf.at[mine(gather)])
        row += held
    load(update, u_v)
    load(piv, m_v)
    load(factor, e_v)

    barrier = pltpu.get_barrier_semaphore()
    for dim in "xzy":
        for offset in (1, 2, 3):
            place = {**at, dim: (at[dim] + offset) % 4}
            pl.semaphore_signal(
                barrier,
                inc=1,
                device_id=(place["y"] * 4 + place["z"], place["x"] * 2 + core),
                device_id_type=pl.DeviceIdType.MESH,
            )
    pl.semaphore_signal(
        barrier, inc=1, device_id=(leaf, at["x"] * 2 + 1 - core), device_id_type=pl.DeviceIdType.MESH
    )
    pl.semaphore_wait(barrier, 10)

    for copy in loads[3:8]:
        copy.wait()
    both(lambda c: [gather.start(c) for gather in hs])
    for copy in loads[:3]:
        copy.wait()
    loads[8].wait()

    def prepare(block, slot):
        high, low = split(d_v[block])
        wide = jnp.concatenate([l_v[block - 1, 0], l_v[block - 1, 1], b_v[block]], axis=1)
        wide_high, wide_low = split(wide)
        first = dot(jnp.concatenate([high, low], axis=0), wide_high)
        product = first[:B] + (first[B:] + dot(high, wide_low))
        g_v[slot] = stack(product[:, : 2 * B])
        c_v[slot] = product[:, 2 * B :]

    def keep(block, value):
        y_v[block] = value
        yhl_v[block] = side(value)

    def couple(block):
        columns = pl.ds(pl.multiple_of(block * B, B), B)
        acc_v[...] += fold(dot(stack(u_v[:, columns]), yhl_v[block]))

    keep(0, fold(dot(stack(d_v[0]), side(b_v[0]))))
    prepare(1, 1)
    acc_v[...] = jnp.zeros_like(acc_v)

    def advance(block, carry):
        slot = lax.rem(block, 2)
        known = jnp.concatenate([yhl_v[block - 1], yhl_v[pattern[block - 1, 1]]], axis=0)
        value = c_v[slot] - fold(dot(g_v[slot], known))
        couple(block - 1)
        prepare(jnp.minimum(block + 1, SB - 1), 1 - slot)
        keep(block, value)
        return carry

    bounds = (1, 7, 13, 19, SB)
    for phase in range(4):
        lax.fori_loop(bounds[phase], bounds[phase + 1], advance, 0)
        if phase < 3:
            both(lambda c: [gather.advance(phase, c) for gather in hs])
    couple(SB - 1)

    stores = []

    def store(source, target):
        copy = pltpu.make_async_copy(source, target, store_sem.at[len(stores)])
        copy.start()
        stores.append(copy)

    def run(gather, before):
        both(gather.start)
        before()
        for phase in range(3):
            both(lambda c: gather.advance(phase, c))
        both(gather.finish)

    def fill(level):
        gather = hs[level - 1]
        both(gather.finish)
        held = HELD[level - 1]
        many = 8 * held
        for y in range(YS[level - 1]):
            for z in range(ZS[level - 1]):
                first = (y * ZS[level - 1] + z) * many
                p_v[first : first + many, :] = gather.buf[y, z].reshape(many, N)

    w0_at = mine(ws[0])
    w0[w0_at] = -acc_v[...]

    def before_first():
        store(y_v, solved_out)
        fill(1)
        loads[9].wait()
        loads[10].wait()

    run(ws[0], before_first)

    w0_blocks = w0.reshape(PB, B, N)

    def landed(entry):
        total = hits[entry, 0] * w0_blocks[spots[entry, 0]]
        for s in range(1, 8):
            total = total + hits[entry, s] * w0_blocks[spots[entry, s]]
        return total

    def place_first(block, carry):
        rows = pl.ds(pl.multiple_of(block * B, B), B)
        p_v[rows, :] = p_v[rows, :] + landed(block)
        return carry

    lax.fori_loop(0, PB, place_first, 0)

    def place(level):
        blocks = ws[level - 1].buf.reshape(2 * PB, B, N)

        def body(block, carry):
            rows = pl.ds(pl.multiple_of(block * B, B), B)
            entry = ENTRY_AT[level] + block
            total = p_v[rows, :]
            for child in (0, 1):
                total = total + hits[entry, child] * blocks[spots[entry, child]]
            p_v[rows, :] = total
            return carry

        lax.fori_loop(0, PB, body, 0)

    def update_rows(level):
        if level == 1:
            return jnp.concatenate([landed(PB), landed(PB + 1)], axis=0)
        held = HELD[level - 1]
        pieces = ws[level - 1].buf.reshape(2 * ROWS // held, held, N)
        entry = ENTRY_AT[level] + PB
        return (
            hits[entry, 0] * pieces[spots[entry, 0]] + hits[entry, 1] * pieces[spots[entry, 1]]
        )

    def multiply(matrix, row, held, chunks):
        tall = min(held, B)
        totals = []
        for first in range(0, held, tall):
            total = None
            column = 0
            for right in chunks:
                depth = right.shape[0]
                left = stack(matrix[row + first : row + first + tall, column : column + depth])
                part = dot(left, right)
                total = part if total is None else total + part
                column += depth
            totals.append(fold(total))
        return totals[0] if len(totals) == 1 else jnp.concatenate(totals, axis=0)

    piv_row = 0
    upd_row = 0
    for level in range(1, LEVELS + 1):
        held = HELD[level - 1]
        value = multiply(m_v, piv_row, held, [side(p_v[...])])
        if level == LEVELS:
            last_v[...] = value
            store(last_v, front_out.at[pl.ds(piv_row, held)])
            break
        gather = zs[level - 1]
        at_own = mine(gather)
        gather.buf[at_own] = value

        def before_solution(level=level, gather=gather, row=piv_row, held=held):
            store(gather.buf.at[mine(gather)], front_out.at[pl.ds(row, held)])
            fill(level + 1)

        run(gather, before_solution)
        chunks = [
            side(gather.buf[y, z].reshape(8 * held, N))
            for y in range(YS[level - 1])
            for z in range(ZS[level - 1])
        ]
        below = update_rows(level) - multiply(e_v, upd_row, held, chunks)
        wide = ws[level]
        wide_at = mine(wide)
        wide.buf[wide_at] = below
        run(wide, lambda: None)
        place(level + 1)
        piv_row += held
        upd_row += held

    both(lambda c: [gather.drain(c) for gather in gathers])
    for copy in stores:
        copy.wait()


def tables(sub_map, front_map):
    leaf = lax.axis_index("leaf")
    front = lax.axis_index("front")
    pivots = jnp.arange(PB, dtype=jnp.int32)
    places, flags = [], []
    maps = lax.dynamic_slice_in_dim(sub_map, leaf * 8, 8)
    wanted = jnp.concatenate([pivots, PB + 2 * front + jnp.arange(2, dtype=jnp.int32)])
    match = maps[None] == wanted[:, None, None]
    places.append(2 * jnp.arange(8, dtype=jnp.int32) + match[:, :, 1].astype(jnp.int32))
    flags.append(match.any(axis=2))
    for level in range(2, LEVELS + 1):
        held = HELD[level - 1]
        maps = lax.dynamic_slice_in_dim(
            front_map, MAP_AT[level - 2] + 2 * (leaf // 2 ** (level - 1)), 2
        )
        row = ((leaf % 2 ** (level - 1)) * 8 + front) * held
        wanted = jnp.concatenate([pivots, (PB + row // B)[None]])
        match = maps[None] == wanted[:, None, None]
        place = jnp.sum(match * jnp.arange(PB, dtype=jnp.int32), axis=2, dtype=jnp.int32)
        place = place + jnp.array([0, PB], jnp.int32)
        last = jnp.arange(PB + 1)[:, None] == PB
        place = jnp.where(last, place * (B // held) + row % B // held, place)
        places.append(jnp.pad(place, ((0, 0), (0, 6))))
        flags.append(jnp.pad(match.any(axis=2), ((0, 0), (0, 6))))
    return jnp.concatenate(places), jnp.concatenate(flags).astype(F32)


def per_device(
    sub_rhs, sub_dinv, sub_off, sub_pattern, sub_update, sub_map,
    front_rhs, piv_inverse, upd_factor, front_map,
):
    def wide(level, held):
        return pltpu.VMEM((YS[level - 1], ZS[level - 1], 4, 2, held, N), F32)

    scratch = [
        pltpu.VMEM((SB, B, N), F32),
        pltpu.VMEM((SB, B, B), F32),
        pltpu.VMEM((SB - 1, K, B, B), F32),
        pltpu.VMEM((2 * B, SB * B), F32),
        pltpu.VMEM((PROWS, ROWS), F32),
        pltpu.VMEM((UROWS, ROWS), F32),
        pltpu.VMEM((SB, B, N), F32),
        pltpu.VMEM((SB, B, 2 * N), BF16),
        pltpu.VMEM((2, 2 * B, 2 * B), BF16),
        pltpu.VMEM((2, B, N), F32),
        pltpu.VMEM((2 * B, N), F32),
        pltpu.VMEM((ROWS, N), F32),
        pltpu.VMEM((HELD[-1], N), F32),
    ]
    scratch += [wide(level, HELD[level - 1]) for level in range(1, 6)]
    scratch += [wide(1, 256)]
    scratch += [wide(level + 1, HELD[level - 1]) for level in range(1, 5)]
    scratch += [wide(level, HELD[level - 1]) for level in range(1, 5)]
    scratch += [
        pltpu.SemaphoreType.DMA((11,)),
        pltpu.SemaphoreType.DMA((6,)),
        pltpu.SemaphoreType.DMA((14, COPIES)),
        pltpu.SemaphoreType.DMA((14, COPIES)),
    ]
    smem = pl.BlockSpec(memory_space=pltpu.SMEM)
    hbm = pl.BlockSpec(memory_space=pl.ANY)
    solved, fronts = pl.pallas_call(
        kernel,
        out_shape=(
            jax.ShapeDtypeStruct((SB, B, N), F32),
            jax.ShapeDtypeStruct((PROWS, N), F32),
        ),
        in_specs=[smem] * 3 + [hbm] * 7,
        out_specs=(hbm, hbm),
        scratch_shapes=scratch,
        compiler_params=pltpu.CompilerParams(
            collective_id=0, has_side_effects=True, vmem_limit_bytes=62 * 2**20
        ),
    )(
        sub_pattern, *tables(sub_map, front_map),
        sub_rhs.reshape(SB, B, N), sub_dinv, sub_off, sub_update, front_rhs, piv_inverse, upd_factor,
    )
    return solved.reshape(SB * B, N), fronts


def solution(mesh):
    rows = P(("leaf", "front"), None)
    return jax.shard_map(
        per_device,
        mesh=mesh,
        in_specs=(
            rows,
            P(("leaf", "front"), None, None),
            P(("leaf", "front"), None, None, None),
            rows,
            rows,
            P(),
            rows,
            rows,
            rows,
            P(),
        ),
        out_specs=(rows, rows),
        check_vma=False,
    )
```

time: 931 us -> 182 us (0.20)
  waiting for transfers between devices: 435 us -> 0 us
  Pallas kernels: 0 us -> 172 us
  matrix products: 136 us -> 0 us
  blocking collectives: 108 us -> 0 us
  loops' own time: 86.4 us -> 0 us
  starting transfers between devices: 50.6 us -> 0 us
  other arithmetic: 48.7 us -> 0.78 us
  local copies, waits for them, and re-layouts: 44.1 us -> 8.09 us
  between operations: 14.7 us -> 1.02 us
    ppermute x26 -> x0, waiting for transfers between devices: 226 us -> none  [swapped(): return lax.ppermute(value, axis, pairs)]
    pallas_call x0 -> x1, Pallas kernels: none -> 172 us  [per_device(): pl.pallas_call(kernel, out_shape=(jax.ShapeDtypeStruct((SB, B, N), F32),...]
    reduce_scatter x5 -> x0, waiting for transfers between devices: 160 us -> none  [per_device(): shared = lax.psum_scatter(buffer, 'front', scatter_dimension=0, tiled=True)]
    dot_general x80 -> x0, matrix products: 136 us -> none  [the longest x23 54.1 us: advance(): jnp.dot(sub_dinv[block_id], remain, precision=highest, preferred_element_...]
    all_gather x7 -> x0, blocking collectives: 108 us -> none  [group_gather(): gathered = lax.all_gather(local_rows, 'front', axis=0, tiled=True)]
    another operation x1 -> x0, loops' own time: 86.4 us -> none  [per_device(): solved = lax.fori_loop(1, SB, advance, solved)]
    ppermute x26 -> x0, starting transfers between devices: 50.3 us -> none  [swapped(): return lax.ppermute(value, axis, pairs)]
    all_gather x2 -> x0, waiting for transfers between devices: 48.7 us -> none  [group_gather(): gathered = lax.all_gather(local_rows, 'front', axis=0, tiled=True)]
  transfers between devices with their start and end apart: 33 -> 0, of which waited for: 33 -> 0; matrix products, arithmetic and copies ran while one was open for 0% -> 0% of each run, Pallas kernels for 0% -> 0%
where the time goes in v1:
time: 182 us
  Pallas kernels  172 us (95%)
  local copies, waits for them, and re-layouts  8.09 us (4%)
    pallas_call x1, Pallas kernels, per_device(): pl.pallas_call(kernel, out_shape=(jax.ShapeDtypeStruct((SB, B, N), F32),...  172 us
    unnamed x7, local copies, waits for them, and re-layouts  5.12 us

profile of v1, /device:TPU:1, one launch (start us, length us, event | category | flops | bytes accessed | tf_op | source)
XLA Modules:
  0.0 181.7 jit_solution(3018084609804084203)
XLA Ops:
  1.0 0.4 copy-done
  1.3 0.1 constant_dynamic-slice_fusion.4
  1.4 0.1 pad_add_fusion.4
  1.5 0.1 pad_add_fusion
  1.6 0.1 fusion.4
  1.7 0.1 bitcast_add_fusion
  1.7 1.4 copy.39.pattern
  3.1 0.9 constant_dynamic-slice_fusion
  4.0 0.1 copy.38
  4.1 0.1 copy.36
  4.2 0.1 copy.35
  4.2 0.1 copy.37
  4.3 0.1 compare_reduce_fusion
  4.4 0.1 fusion.2
  4.5 0.1 compare_reduce_fusion.2
  4.6 0.1 fusion
  4.7 0.1 add_select_fusion.1
  4.8 0.1 concatenate.27
  5.0 0.1 concatenate.26
  5.1 0.7 copy.40.spots
  5.8 0.7 copy.41.hits
  6.5 171.8 %shard_map.149 = (f32[24,128,128]{2,1,0:T(8,128)}, f32[496,128]{1,0:T(8,128)}) custom-call(s32[23,2]{1,0:T(8,128)} %copy.39.pattern, s32[86,8]{1,0:T(8,128)} %copy.40.spots, f32[86,8]{1,0:T(8,128)} %copy.41.hits, f32[24,128,128]{2,1,0:T(8,128)} %bitcast.9, f32[24,128,128]{2,1,0:T(8,128)} %dinv.1, f32[23,2,128,128]{3,2,1,0:T(8,128)} %off.1, ...), custom_call_target="tpu_custom_call" | custom-call | tf_op jit(solution)/shard_map/pallas_call | solution.py:445
  178.3 2.7 %copy.44 = f32[3072,128]{1,0:T(8,128)} copy(f32[3072,128]{1,0:T(8,128)} %bitcast.8) | data formatting | bytes 3145728
  181.0 0.7 copy.45
  (18 shorter events, 0.1 us)
Async XLA Ops:
  0.6 0.7 copy-start
  178.3 2.7 %copy-start.1 = (f32[496,128]{1,0:T(8,128)S(1)}, f32[496,128]{1,0:T(8,128)}, u32[]{:S(2)}) copy-start(f32[496,128]{1,0:T(8,128)} %get-tuple-element.31) | copy-start | bytes 761860

commit v2 on v1

--- a/solution.py
+++ b/solution.py
@@ -1,3 +1,5 @@
+import itertools
+
 import jax
 import jax.numpy as jnp
 from jax import lax
@@ -20,9 +22,11 @@
 HELD = (256, 128, 64, 32, 16)
 MAP_AT = (0, 16, 24, 28)
 ENTRY_AT = (None, 0, 18, 35, 52, 69)
-ORDER = ("xzy", "yzx")
-DIM_AT = {"x": 0, "z": 3, "y": 6}
-COPIES = 19
+MIXED = (("x", "zy"), ("zy", "x"))
+SAME = (("x", "zy"), ("x", "zy"))
+CROSS = 18
+COPIES = CROSS + 19
+COLUMNS_AT = 86
 F32 = jnp.float32
 BF16 = jnp.bfloat16
 
@@ -50,28 +54,41 @@
 
 
 class Gather:
-    def __init__(self, buf, send, recv, level, at):
+    def __init__(self, buf, send, recv, level, at, order, eager):
         self.buf, self.send, self.recv, self.at = buf, send, recv, at
         self.size = {"x": 4, "z": ZS[level - 1], "y": YS[level - 1]}
-        self.own = {
-            d: 0 if self.size[d] == 1 else at[d] % self.size[d] for d in "yzx"
-        }
-
-    def dims(self, core):
-        return [d for d in ORDER[core] if self.size[d] > 1]
-
-    def view(self, full, own, core):
-        index = [slice(None) if d in full else own[d] for d in "yzx"]
-        return self.buf.at[index[0], index[1], index[2], core]
-
-    def offsets(self, dim):
-        return (2, 1, 3) if self.size[dim] == 4 else (1,)
+        self.order, self.eager = order, eager
+        self.own = {d: 0 if self.size[d] == 1 else at[d] % self.size[d] for d in "yzx"}
+
+    def sets(self, core):
+        found = ["".join(d for d in dims if self.size[d] > 1) for dims in self.order[core]]
+        return found[0] or found[1], found[1] if found[0] else ""
+
+    def hops(self, dims):
+        steps = [
+            dict(zip(dims, offsets))
+            for offsets in itertools.product(*(range(self.size[d]) for d in dims))
+            if any(offsets)
+        ]
+        return sorted(steps, key=lambda step: sum(min(o, self.size[d] - o) for d, o in step.items()))
 
     def moved(self, dim, offset):
         here = self.at[dim]
+        if offset == 0:
+            return here
         if self.size[dim] == 4:
             return (here + offset) % 4
         return here + 1 - 2 * (here % 2)
+
+    def origin(self, step):
+        return {
+            d: self.moved(d, -o % self.size[d]) % self.size[d] for d, o in step.items()
+        }
+
+    def view(self, core, full="", **places):
+        place = {**self.own, **places}
+        index = [slice(None) if d in full else place[d] for d in "yzx"]
+        return self.buf.at[index[0], index[1], index[2], core]
 
     def copy(self, view, which, **changes):
         place = {**self.at, **changes}
@@ -84,71 +101,83 @@
             device_id_type=pl.DeviceIdType.MESH,
         )
 
-    def outgoing(self, phase, core):
-        dims = self.dims(core)
-        dim = dims[phase]
-        view = self.view(dims[:phase], self.own, core)
-        return [
-            self.copy(view, DIM_AT[dim] + offset - 1, core=core, **{dim: self.moved(dim, offset)})
-            for offset in self.offsets(dim)
-        ]
-
-    def incoming(self, phase, core):
-        dims = self.dims(core)
-        dim = dims[phase]
-        found = []
-        for offset in self.offsets(dim):
-            origin = self.moved(dim, 4 - offset) % self.size[dim]
-            view = self.view(dims[:phase], {**self.own, dim: origin}, core)
-            found.append((view, DIM_AT[dim] + offset - 1))
-        return found
-
-    def shared(self, core):
-        views = [self.view((), self.own, core)]
-        for phase in range(len(self.dims(core))):
-            views += [view for view, _ in self.incoming(phase, core)]
-        return views
-
-    def crossing(self, core, to, first=0, many=COPIES):
-        views = list(enumerate(self.shared(core)))[first : first + many]
-        return [self.copy(view, 9 + which, core=to) for which, view in views]
-
-    def start(self, core):
-        for copy in self.outgoing(0, core):
-            copy.start()
-        for copy in self.crossing(core, 1 - core, 0, 1):
-            copy.start()
-
-    def phases(self, core):
-        return len(self.dims(core))
-
-    def advance(self, phase, core):
-        if phase >= self.phases(core):
-            return
-        first = 1 + sum(len(self.incoming(p, core)) for p in range(phase))
-        arrivals = self.incoming(phase, core)
-        for view, which in arrivals:
+    def to(self, step):
+        return {d: self.moved(d, o) for d, o in step.items()}
+
+    def out(self, view, which, core, step):
+        return lambda: self.copy(view, which, core=core, **self.to(step))
+
+    def across(self, view, which, core):
+        return lambda: self.copy(view, which, core=1 - core)
+
+    def plan(self, core):
+        first, second = self.sets(core)
+        near, far = self.hops(first), self.hops(second) if second else []
+        cross = CROSS
+        begin = [self.out(self.view(core), i, core, step) for i, step in enumerate(near)]
+        used = len(near)
+        mine = [(self.view(core), cross)]
+        middle, close = [], []
+        held = [{}] + [self.origin(step) for step in near]
+        sets = [held[i : i + 1] for i in range(len(held))] if self.eager else [held]
+        sends = []
+        for group in sets:
+            view = self.view(core, **group[0]) if self.eager else self.view(core, first)
+            sends.append([self.out(view, used + j, core, step) for j, step in enumerate(far)])
+            used += len(far)
+        if self.eager:
+            begin += sends[0]
+        for i, step in enumerate(near):
+            view = self.view(core, **held[i + 1])
+            mine.append((view, cross + 1 + i))
+            after = sends[i + 1] if self.eager else sends[0] if i == len(near) - 1 else []
+            middle.append(([(view, i)], after + [self.across(view, cross + 1 + i, core)]))
+        if not second:
+            middle = [(wait, [start[-1]]) for wait, start in middle]
+        for j, step in enumerate(far):
+            origin = self.origin(step)
+            waits = []
+            for g, group in enumerate(sets):
+                if self.eager:
+                    view = self.view(core, **{**group[0], **origin})
+                else:
+                    view = self.view(core, first, **origin)
+                waits.append((view, len(near) + g * len(far) + j))
+            view, which = self.view(core, first, **origin), cross + 1 + len(near) + j
+            mine.append((view, which))
+            close.append((waits, [self.across(view, which, core)]))
+        begin.append(self.across(self.view(core), cross, core))
+        return begin, middle, close, mine
+
+    def begin(self, core):
+        for make in self.plan(core)[0]:
+            make().start()
+
+    def follow(self, steps, core):
+        for waits, starts in steps:
+            for view, which in waits:
+                self.copy(view, which, core=1 - core).wait_recv()
+            for make in starts:
+                make().start()
+
+    def middle(self, core):
+        self.follow(self.plan(core)[1], core)
+
+    def close(self, core):
+        self.follow(self.plan(core)[2], core)
+
+    def finish(self, core):
+        for view, which in self.plan(1 - core)[3]:
             self.copy(view, which, core=1 - core).wait_recv()
-        if phase + 1 < self.phases(core):
-            for copy in self.outgoing(phase + 1, core):
-                copy.start()
-        for copy in self.crossing(core, 1 - core, first, len(arrivals)):
-            copy.start()
-
-    def finish(self, core):
-        for copy in self.crossing(1 - core, 1 - core):
-            copy.wait_recv()
 
     def drain(self, core):
-        for phase in range(self.phases(core)):
-            for copy in self.outgoing(phase, core):
-                copy.wait_send()
-        for copy in self.crossing(core, 1 - core):
-            copy.wait_send()
+        begin, middle, close, _ = self.plan(core)
+        for make in begin + [make for _, starts in middle + close for make in starts]:
+            make().wait_send()
 
 
 def kernel(
-    pattern, spots, hits,
+    table,
     rhs, dinv, off, update, front_rhs, piv, factor,
     solved_out, front_out,
     b_v, d_v, l_v, u_v, m_v, e_v, y_v, yhl_v, g_v, c_v, acc_v, p_v, last_v,
@@ -169,7 +198,7 @@
     bufs = (h1, h2, h3, h4, h5, w0, w1, w2, w3, w4, z1, z2, z3, z4)
     groups = (1, 2, 3, 4, 5, 1, 2, 3, 4, 5, 1, 2, 3, 4)
     gathers = [
-        Gather(buf, send.at[g], recv.at[g], level, at)
+        Gather(buf, send.at[g], recv.at[g], level, at, SAME if g < 5 else MIXED, level < 4)
         for g, (buf, level) in enumerate(zip(bufs, groups))
     ]
     hs, ws, zs = gathers[:5], gathers[5:10], gathers[10:]
@@ -197,23 +226,23 @@
     load(factor, e_v)
 
     barrier = pltpu.get_barrier_semaphore()
-    for dim in "xzy":
-        for offset in (1, 2, 3):
-            place = {**at, dim: (at[dim] + offset) % 4}
-            pl.semaphore_signal(
-                barrier,
-                inc=1,
-                device_id=(place["y"] * 4 + place["z"], place["x"] * 2 + core),
-                device_id_type=pl.DeviceIdType.MESH,
-            )
-    pl.semaphore_signal(
-        barrier, inc=1, device_id=(leaf, at["x"] * 2 + 1 - core), device_id_type=pl.DeviceIdType.MESH
-    )
-    pl.semaphore_wait(barrier, 10)
+    peers = [(at["y"], at["z"], (at["x"] + o) % 4, core) for o in (1, 2, 3)]
+    peers += [
+        ((at["y"] + oy) % 4, (at["z"] + oz) % 4, at["x"], core)
+        for oy in range(4)
+        for oz in range(4)
+        if oy or oz
+    ]
+    peers.append((at["y"], at["z"], at["x"], 1 - core))
+    for y, z, x, c in peers:
+        pl.semaphore_signal(
+            barrier, inc=1, device_id=(y * 4 + z, x * 2 + c), device_id_type=pl.DeviceIdType.MESH
+        )
+    pl.semaphore_wait(barrier, len(peers))
 
     for copy in loads[3:8]:
         copy.wait()
-    both(lambda c: [gather.start(c) for gather in hs])
+    both(lambda c: [gather.begin(c) for gather in hs])
     for copy in loads[:3]:
         copy.wait()
     loads[8].wait()
@@ -241,18 +270,16 @@
 
     def advance(block, carry):
         slot = lax.rem(block, 2)
-        known = jnp.concatenate([yhl_v[block - 1], yhl_v[pattern[block - 1, 1]]], axis=0)
+        known = jnp.concatenate([yhl_v[block - 1], yhl_v[table[COLUMNS_AT + block - 1, 0]]], axis=0)
         value = c_v[slot] - fold(dot(g_v[slot], known))
         couple(block - 1)
         prepare(jnp.minimum(block + 1, SB - 1), 1 - slot)
         keep(block, value)
         return carry
 
-    bounds = (1, 7, 13, 19, SB)
-    for phase in range(4):
-        lax.fori_loop(bounds[phase], bounds[phase + 1], advance, 0)
-        if phase < 3:
-            both(lambda c: [gather.advance(phase, c) for gather in hs])
+    lax.fori_loop(1, 17, advance, 0)
+    both(lambda c: [gather.middle(c) for gather in hs])
+    lax.fori_loop(17, SB, advance, 0)
     couple(SB - 1)
 
     stores = []
@@ -263,15 +290,24 @@
         stores.append(copy)
 
     def run(gather, before):
-        both(gather.start)
+        both(gather.begin)
         before()
-        for phase in range(3):
-            both(lambda c: gather.advance(phase, c))
-        both(gather.finish)
+
+        def rest(c):
+            gather.middle(c)
+            gather.close(c)
+            gather.finish(c)
+
+        both(rest)
 
     def fill(level):
         gather = hs[level - 1]
-        both(gather.finish)
+
+        def rest(c):
+            gather.close(c)
+            gather.finish(c)
+
+        both(rest)
         held = HELD[level - 1]
         many = 8 * held
         for y in range(YS[level - 1]):
@@ -290,12 +326,15 @@
 
     run(ws[0], before_first)
 
+    def hit(entry, which):
+        return table[entry, 8 + which].astype(F32)
+
     w0_blocks = w0.reshape(PB, B, N)
 
     def landed(entry):
-        total = hits[entry, 0] * w0_blocks[spots[entry, 0]]
+        total = hit(entry, 0) * w0_blocks[table[entry, 0]]
         for s in range(1, 8):
-            total = total + hits[entry, s] * w0_blocks[spots[entry, s]]
+            total = total + hit(entry, s) * w0_blocks[table[entry, s]]
         return total
 
     def place_first(block, carry):
@@ -313,7 +352,7 @@
             entry = ENTRY_AT[level] + block
             total = p_v[rows, :]
             for child in (0, 1):
-                total = total + hits[entry, child] * blocks[spots[entry, child]]
+                total = total + hit(entry, child) * blocks[table[entry, child]]
             p_v[rows, :] = total
             return carry
 
@@ -326,7 +365,7 @@
         pieces = ws[level - 1].buf.reshape(2 * ROWS // held, held, N)
         entry = ENTRY_AT[level] + PB
         return (
-            hits[entry, 0] * pieces[spots[entry, 0]] + hits[entry, 1] * pieces[spots[entry, 1]]
+            hit(entry, 0) * pieces[table[entry, 0]] + hit(entry, 1) * pieces[table[entry, 1]]
         )
 
     def multiply(matrix, row, held, chunks):
@@ -381,7 +420,7 @@
         copy.wait()
 
 
-def tables(sub_map, front_map):
+def tables(sub_pattern, sub_map, front_map):
     leaf = lax.axis_index("leaf")
     front = lax.axis_index("front")
     pivots = jnp.arange(PB, dtype=jnp.int32)
@@ -405,7 +444,8 @@
         place = jnp.where(last, place * (B // held) + row % B // held, place)
         places.append(jnp.pad(place, ((0, 0), (0, 6))))
         flags.append(jnp.pad(match.any(axis=2), ((0, 0), (0, 6))))
-    return jnp.concatenate(places), jnp.concatenate(flags).astype(F32)
+    found = jnp.concatenate([jnp.concatenate(places), jnp.concatenate(flags).astype(jnp.int32)], axis=1)
+    return jnp.concatenate([found, jnp.pad(sub_pattern[:, 1:], ((0, 0), (0, 15)))])
 
 
 def per_device(
@@ -448,14 +488,14 @@
             jax.ShapeDtypeStruct((SB, B, N), F32),
             jax.ShapeDtypeStruct((PROWS, N), F32),
         ),
-        in_specs=[smem] * 3 + [hbm] * 7,
+        in_specs=[smem] + [hbm] * 7,
         out_specs=(hbm, hbm),
         scratch_shapes=scratch,
         compiler_params=pltpu.CompilerParams(
             collective_id=0, has_side_effects=True, vmem_limit_bytes=62 * 2**20
         ),
     )(
-        sub_pattern, *tables(sub_map, front_map),
+        tables(sub_pattern, sub_map, front_map),
         sub_rhs.reshape(SB, B, N), sub_dinv, sub_off, sub_update, front_rhs, piv_inverse, upd_factor,
     )
     return solved.reshape(SB * B, N), fronts

time: 182 us -> 155 us (0.85)
  Pallas kernels: 172 us -> 147 us
    pallas_call x1, Pallas kernels: 172 us -> 147 us  [per_device(): pl.pallas_call(kernel, out_shape=(jax.ShapeDtypeStruct((SB, B, N), F32),...]
    unnamed x7 -> x6, local copies, waits for them, and re-layouts: 5.12 us -> 3.4 us
where the time goes in v2:
time: 155 us
  Pallas kernels  147 us (95%)
  local copies, waits for them, and re-layouts  6.35 us (4%)
    pallas_call x1, Pallas kernels, per_device(): pl.pallas_call(kernel, out_shape=(jax.ShapeDtypeStruct((SB, B, N), F32),...  147 us
    unnamed x6, local copies, waits for them, and re-layouts  3.4 us

profile of v2, /device:TPU:1, one launch (start us, length us, event | category | flops | bytes accessed | tf_op | source)
XLA Modules:
  0.0 154.9 jit_solution(5131081018911117217)
XLA Ops:
  0.6 0.0 copy-start
  1.0 0.7 slice.7
  1.6 0.1 constant_dynamic-slice_fusion.4
  1.7 0.1 pad_add_fusion.5
  1.8 0.1 pad_add_fusion.1
  1.9 0.1 broadcast_compare_fusion
  2.0 0.1 bitcast_add_fusion
  2.1 0.9 constant_dynamic-slice_fusion
  3.0 0.1 copy.29
  3.0 0.1 copy.27
  3.1 0.1 copy.26
  3.2 0.1 copy.28
  3.3 0.1 compare_reduce_fusion
  3.4 0.1 fusion.2
  3.5 0.1 compare_reduce_fusion.2
  3.6 0.1 fusion
  3.7 0.1 add_select_fusion.1
  3.8 0.1 concatenate.33
  3.9 0.1 concatenate.32
  4.0 0.1 pad_add_fusion
  4.1 0.7 copy.30.table
  4.8 146.7 %shard_map.149 = (f32[24,128,128]{2,1,0:T(8,128)}, f32[496,128]{1,0:T(8,128)}) custom-call(s32[109,16]{1,0:T(8,128)} %copy.30.table, f32[24,128,128]{2,1,0:T(8,128)} %bitcast.8, f32[24,128,128]{2,1,0:T(8,128)} %dinv.1, f32[23,2,128,128]{3,2,1,0:T(8,128)} %off.1, f32[256,3072]{1,0:T(8,128)} %update.1, f32[496,128]{1,0:T(8,128)} %front_rhs.1, ...), custom_call_target="tpu_custom_call" | custom-call | tf_op jit(solution)/shard_map/pallas_call | solution.py:485
  151.5 2.7 %copy.33 = f32[3072,128]{1,0:T(8,128)} copy(f32[3072,128]{1,0:T(8,128)} %bitcast.9) | data formatting | bytes 3145728
  154.2 0.7 copy.34
  (18 shorter events, 0.1 us)
Async XLA Ops:
  0.6 1.0 copy-start
  151.5 2.7 %copy-start.1 = (f32[496,128]{1,0:T(8,128)S(1)}, f32[496,128]{1,0:T(8,128)}, u32[]{:S(2)}) copy-start(f32[496,128]{1,0:T(8,128)} %get-tuple-element.31) | copy-start | bytes 761860

commit v3 on v2

--- a/solution.py
+++ b/solution.py
@@ -27,6 +27,7 @@
 CROSS = 18
 COPIES = CROSS + 19
 COLUMNS_AT = 86
+EARLY = 8
 F32 = jnp.float32
 BF16 = jnp.bfloat16
 
@@ -214,14 +215,16 @@
         copy.start()
         loads.append(copy)
 
-    load(dinv, d_v)
-    load(off, l_v)
-    load(rhs, b_v)
     row = 0
     for gather, held in zip(hs, HELD):
         load(front_rhs.at[pl.ds(row, held)], gather.buf.at[mine(gather)])
         row += held
-    load(update, u_v)
+    for first, many in ((0, EARLY), (EARLY, SB - EARLY)):
+        load(dinv.at[pl.ds(first, many)], d_v.at[pl.ds(first, many)])
+        load(off.at[pl.ds(first, many - first // EARLY)], l_v.at[pl.ds(first, many - first // EARLY)])
+        load(rhs.at[pl.ds(first, many)], b_v.at[pl.ds(first, many)])
+        columns = pl.ds(first * B, many * B)
+        load(update.at[:, columns], u_v.at[:, columns])
     load(piv, m_v)
     load(factor, e_v)
 
@@ -240,12 +243,11 @@
         )
     pl.semaphore_wait(barrier, len(peers))
 
-    for copy in loads[3:8]:
+    for copy in loads[:5]:
         copy.wait()
     both(lambda c: [gather.begin(c) for gather in hs])
-    for copy in loads[:3]:
+    for copy in loads[5:9]:
         copy.wait()
-    loads[8].wait()
 
     def prepare(block, slot):
         high, low = split(d_v[block])
@@ -277,9 +279,10 @@
         keep(block, value)
         return carry
 
-    lax.fori_loop(1, 17, advance, 0)
-    both(lambda c: [gather.middle(c) for gather in hs])
-    lax.fori_loop(17, SB, advance, 0)
+    lax.fori_loop(1, EARLY - 1, advance, 0)
+    for copy in loads[9:13]:
+        copy.wait()
+    lax.fori_loop(EARLY - 1, SB, advance, 0)
     couple(SB - 1)
 
     stores = []
@@ -319,10 +322,11 @@
     w0[w0_at] = -acc_v[...]
 
     def before_first():
+        both(lambda c: [gather.middle(c) for gather in hs])
         store(y_v, solved_out)
         fill(1)
-        loads[9].wait()
-        loads[10].wait()
+        loads[13].wait()
+        loads[14].wait()
 
     run(ws[0], before_first)
 
@@ -475,7 +479,7 @@
     scratch += [wide(level + 1, HELD[level - 1]) for level in range(1, 5)]
     scratch += [wide(level, HELD[level - 1]) for level in range(1, 5)]
     scratch += [
-        pltpu.SemaphoreType.DMA((11,)),
+        pltpu.SemaphoreType.DMA((15,)),
         pltpu.SemaphoreType.DMA((6,)),
         pltpu.SemaphoreType.DMA((14, COPIES)),
         pltpu.SemaphoreType.DMA((14, COPIES)),

time: 155 us -> 149 us (0.961)
  Pallas kernels: 147 us -> 140 us
    pallas_call x1, Pallas kernels: 147 us -> 140 us  [per_device(): pl.pallas_call(kernel, out_shape=(jax.ShapeDtypeStruct((SB, B, N), F32),...]
where the time goes in v3:
time: 149 us; the launch traced here: 148 us
  Pallas kernels  140 us (94%)
  local copies, waits for them, and re-layouts  6.35 us (4%)
    pallas_call x1, Pallas kernels, per_device(): pl.pallas_call(kernel, out_shape=(jax.ShapeDtypeStruct((SB, B, N), F32),...  140 us
    unnamed x6, local copies, waits for them, and re-layouts  3.4 us

profile of v3, /device:TPU:1, one launch (start us, length us, event | category | flops | bytes accessed | tf_op | source)
XLA Modules:
  0.0 148.2 jit_solution(16729366853970416301)
XLA Ops:
  0.6 0.0 copy-start
  1.0 0.7 slice.7
  1.6 0.1 constant_dynamic-slice_fusion.4
  1.7 0.1 pad_add_fusion.5
  1.8 0.1 pad_add_fusion.1
  1.9 0.1 broadcast_compare_fusion
  2.0 0.1 bitcast_add_fusion
  2.1 0.9 constant_dynamic-slice_fusion
  3.0 0.1 copy.29
  3.0 0.1 copy.27
  3.1 0.1 copy.26
  3.2 0.1 copy.28
  3.3 0.1 compare_reduce_fusion
  3.4 0.1 fusion.2
  3.5 0.1 compare_reduce_fusion.2
  3.6 0.1 fusion
  3.7 0.1 add_select_fusion.1
  3.8 0.1 concatenate.33
  3.9 0.1 concatenate.32
  4.0 0.1 pad_add_fusion
  4.1 0.7 copy.30.table
  4.8 140.0 %shard_map.149 = (f32[24,128,128]{2,1,0:T(8,128)}, f32[496,128]{1,0:T(8,128)}) custom-call(s32[109,16]{1,0:T(8,128)} %copy.30.table, f32[24,128,128]{2,1,0:T(8,128)} %bitcast.8, f32[24,128,128]{2,1,0:T(8,128)} %dinv.1, f32[23,2,128,128]{3,2,1,0:T(8,128)} %off.1, f32[256,3072]{1,0:T(8,128)} %update.1, f32[496,128]{1,0:T(8,128)} %front_rhs.1, ...), custom_call_target="tpu_custom_call" | custom-call | tf_op jit(solution)/shard_map/pallas_call | solution.py:489
  144.8 2.7 %copy.33 = f32[3072,128]{1,0:T(8,128)} copy(f32[3072,128]{1,0:T(8,128)} %bitcast.9) | data formatting | bytes 3145728
  147.5 0.7 copy.34
  (18 shorter events, 0.1 us)
Async XLA Ops:
  0.6 1.0 copy-start
  144.8 2.7 %copy-start.1 = (f32[496,128]{1,0:T(8,128)S(1)}, f32[496,128]{1,0:T(8,128)}, u32[]{:S(2)}) copy-start(f32[496,128]{1,0:T(8,128)} %get-tuple-element.31) | copy-start | bytes 761860

commit v4 on v2

--- a/solution.py
+++ b/solution.py
@@ -24,9 +24,11 @@
 ENTRY_AT = (None, 0, 18, 35, 52, 69)
 MIXED = (("x", "zy"), ("zy", "x"))
 SAME = (("x", "zy"), ("x", "zy"))
-CROSS = 18
-COPIES = CROSS + 19
+SENDS = (3, 7, 15, 10, 18)
+COPIES = (7, 12, 22, 21, 37)
+HALF = 64
 COLUMNS_AT = 86
+EARLY = 8
 F32 = jnp.float32
 BF16 = jnp.bfloat16
 
@@ -53,9 +55,50 @@
     return product[:half, :N] + (product[:half, N:] + product[half:, :N])
 
 
+def low_half(shape):
+    return lax.broadcasted_iota(jnp.int32, shape, len(shape) - 1) < HALF
+
+
+def turned(value):
+    return pltpu.roll(value, HALF, 1)
+
+
+def merged(left, right):
+    return jnp.where(low_half(left.shape), left, turned(right))
+
+
+def pack(value):
+    rows = value.shape[0]
+    unit = min(rows, B)
+    parts = []
+    for first in range(0, rows, unit):
+        middle = first + unit // 2
+        parts.append(merged(value[first:middle], value[middle : first + unit]))
+    return parts[0] if len(parts) == 1 else jnp.concatenate(parts, axis=0)
+
+
+def unpack(value, unit):
+    rows = value.shape[0]
+    shape = (2 * rows // unit, unit // 2, N)
+    pair = jnp.concatenate([value.reshape(shape), turned(value).reshape(shape)], axis=1)
+    return pair.reshape(2 * rows, N)
+
+
+def narrow(value):
+    high = value.astype(BF16).astype(F32)
+    return merged(high, value - high).astype(BF16)
+
+
+def fold_narrow(product):
+    half = product.shape[0] // 2
+    top = product[:half]
+    return top + (turned(top) + product[half:])
+
+
 class Gather:
-    def __init__(self, buf, send, recv, level, at, order, eager):
+    def __init__(self, buf, send, recv, base, level, at, order):
         self.buf, self.send, self.recv, self.at = buf, send, recv, at
+        self.base, self.level, eager = base, level, level < 4
         self.size = {"x": 4, "z": ZS[level - 1], "y": YS[level - 1]}
         self.order, self.eager = order, eager
         self.own = {d: 0 if self.size[d] == 1 else at[d] % self.size[d] for d in "yzx"}
@@ -95,8 +138,8 @@
         return pltpu.make_async_remote_copy(
             src_ref=view,
             dst_ref=view,
-            send_sem=self.send.at[which],
-            recv_sem=self.recv.at[which],
+            send_sem=self.send.at[self.base + which],
+            recv_sem=self.recv.at[self.base + which],
             device_id=(place["y"] * 4 + place["z"], place["x"] * 2 + place["core"]),
             device_id_type=pl.DeviceIdType.MESH,
         )
@@ -113,7 +156,7 @@
     def plan(self, core):
         first, second = self.sets(core)
         near, far = self.hops(first), self.hops(second) if second else []
-        cross = CROSS
+        cross = SENDS[self.level - 1]
         begin = [self.out(self.view(core), i, core, step) for i, step in enumerate(near)]
         used = len(near)
         mine = [(self.view(core), cross)]
@@ -180,9 +223,8 @@
     table,
     rhs, dinv, off, update, front_rhs, piv, factor,
     solved_out, front_out,
-    b_v, d_v, l_v, u_v, m_v, e_v, y_v, yhl_v, g_v, c_v, acc_v, p_v, last_v,
-    h1, h2, h3, h4, h5, w0, w1, w2, w3, w4, z1, z2, z3, z4,
-    load_sem, store_sem, send, recv,
+    b_v, d_v, l_v, u_v, m_v, e_v, y_v, yhl_v, g_v, c_v, acc_v, p_v, ms_v, es_v, z_v,
+    h1, h2, h3, h4, h5, *rest,
 ):
     leaf = lax.axis_index("leaf")
     front = lax.axis_index("front")
@@ -195,13 +237,17 @@
             def _():
                 step(which)
 
-    bufs = (h1, h2, h3, h4, h5, w0, w1, w2, w3, w4, z1, z2, z3, z4)
-    groups = (1, 2, 3, 4, 5, 1, 2, 3, 4, 5, 1, 2, 3, 4)
-    gathers = [
-        Gather(buf, send.at[g], recv.at[g], level, at, SAME if g < 5 else MIXED, level < 4)
-        for g, (buf, level) in enumerate(zip(bufs, groups))
-    ]
-    hs, ws, zs = gathers[:5], gathers[5:10], gathers[10:]
+    streams, (load_sem, store_sem, send, recv) = rest[:18], rest[18:]
+    levels = [1, 2, 3, 4, 5] + 2 * [1, 2, 3, 4, 5, 1, 2, 3, 4]
+    gathers = []
+    base = 0
+    for buf, level in zip((h1, h2, h3, h4, h5, *streams), levels):
+        order = SAME if len(gathers) < 5 else MIXED
+        gathers.append(Gather(buf, send, recv, base, level, at, order))
+        base += COPIES[level - 1]
+    hs = gathers[:5]
+    ws = (gathers[5:10], gathers[14:19])
+    zs = (gathers[10:14], gathers[19:23])
 
     def mine(gather):
         own = gather.own
@@ -214,14 +260,16 @@
         copy.start()
         loads.append(copy)
 
-    load(dinv, d_v)
-    load(off, l_v)
-    load(rhs, b_v)
     row = 0
     for gather, held in zip(hs, HELD):
         load(front_rhs.at[pl.ds(row, held)], gather.buf.at[mine(gather)])
         row += held
-    load(update, u_v)
+    for first, many in ((0, EARLY), (EARLY, SB - EARLY)):
+        load(dinv.at[pl.ds(first, many)], d_v.at[pl.ds(first, many)])
+        load(off.at[pl.ds(first, many - first // EARLY)], l_v.at[pl.ds(first, many - first // EARLY)])
+        load(rhs.at[pl.ds(first, many)], b_v.at[pl.ds(first, many)])
+        columns = pl.ds(first * B, many * B)
+        load(update.at[:, columns], u_v.at[:, columns])
     load(piv, m_v)
     load(factor, e_v)
 
@@ -240,12 +288,11 @@
         )
     pl.semaphore_wait(barrier, len(peers))
 
-    for copy in loads[3:8]:
+    for copy in loads[:5]:
         copy.wait()
     both(lambda c: [gather.begin(c) for gather in hs])
-    for copy in loads[:3]:
+    for copy in loads[5:9]:
         copy.wait()
-    loads[8].wait()
 
     def prepare(block, slot):
         high, low = split(d_v[block])
@@ -277,9 +324,10 @@
         keep(block, value)
         return carry
 
-    lax.fori_loop(1, 17, advance, 0)
-    both(lambda c: [gather.middle(c) for gather in hs])
-    lax.fori_loop(17, SB, advance, 0)
+    lax.fori_loop(1, EARLY - 1, advance, 0)
+    for copy in loads[9:13]:
+        copy.wait()
+    lax.fori_loop(EARLY - 1, SB, advance, 0)
     couple(SB - 1)
 
     stores = []
@@ -289,16 +337,10 @@
         copy.start()
         stores.append(copy)
 
-    def run(gather, before):
-        both(gather.begin)
-        before()
-
-        def rest(c):
-            gather.middle(c)
-            gather.close(c)
-            gather.finish(c)
-
-        both(rest)
+    def widen(source, target, level, row, held):
+        tall = min(held, B)
+        for first in range(row, row + held, tall):
+            target[2 * first : 2 * (first + tall), :] = stack(source[first : first + tall, :])
 
     def fill(level):
         gather = hs[level - 1]
@@ -313,107 +355,141 @@
         for y in range(YS[level - 1]):
             for z in range(ZS[level - 1]):
                 first = (y * ZS[level - 1] + z) * many
-                p_v[first : first + many, :] = gather.buf[y, z].reshape(many, N)
-
-    w0_at = mine(ws[0])
-    w0[w0_at] = -acc_v[...]
-
-    def before_first():
-        store(y_v, solved_out)
-        fill(1)
-        loads[9].wait()
-        loads[10].wait()
-
-    run(ws[0], before_first)
+                part = gather.buf[y, z].reshape(many, N)
+                p_v[0, first : first + many, :] = part
+                p_v[1, first : first + many, :] = turned(part)
+
+    def send_update(stream, level, value):
+        gather = ws[stream][level]
+        own = mine(gather)
+        gather.buf[own] = pack(value)
+        both(gather.begin)
 
     def hit(entry, which):
         return table[entry, 8 + which].astype(F32)
 
-    w0_blocks = w0.reshape(PB, B, N)
-
-    def landed(entry):
-        total = hit(entry, 0) * w0_blocks[table[entry, 0]]
-        for s in range(1, 8):
-            total = total + hit(entry, s) * w0_blocks[table[entry, s]]
+    def landed(stream, level, entry):
+        gather = ws[stream][level - 1]
+        blocks = gather.buf.reshape(PB if level == 1 else 2 * PB, HALF, N)
+        total = hit(entry, 0) * blocks[table[entry, 0]]
+        for child in range(1, 8 if level == 1 else 2):
+            total = total + hit(entry, child) * blocks[table[entry, child]]
         return total
 
-    def place_first(block, carry):
-        rows = pl.ds(pl.multiple_of(block * B, B), B)
-        p_v[rows, :] = p_v[rows, :] + landed(block)
-        return carry
-
-    lax.fori_loop(0, PB, place_first, 0)
-
-    def place(level):
-        blocks = ws[level - 1].buf.reshape(2 * PB, B, N)
+    def place(stream, level):
+        unit = B if level == 1 else min(B, HELD[level - 2])
 
         def body(block, carry):
             rows = pl.ds(pl.multiple_of(block * B, B), B)
-            entry = ENTRY_AT[level] + block
-            total = p_v[rows, :]
-            for child in (0, 1):
-                total = total + hit(entry, child) * blocks[table[entry, child]]
-            p_v[rows, :] = total
+            total = unpack(landed(stream, level, ENTRY_AT[level] + block), unit)
+            p_v[stream, rows, :] = p_v[stream, rows, :] + total
             return carry
 
         lax.fori_loop(0, PB, body, 0)
 
-    def update_rows(level):
+    def update_rows(stream, level):
+        entry = ENTRY_AT[level] + PB
         if level == 1:
-            return jnp.concatenate([landed(PB), landed(PB + 1)], axis=0)
+            parts = [unpack(landed(stream, 1, entry + i), B) for i in (0, 1)]
+            return jnp.concatenate(parts, axis=0)
+        if level == 2:
+            return unpack(landed(stream, 2, entry), B)
         held = HELD[level - 1]
-        pieces = ws[level - 1].buf.reshape(2 * ROWS // held, held, N)
-        entry = ENTRY_AT[level] + PB
-        return (
+        pieces = ws[stream][level - 1].buf.reshape(ROWS // held, held, N)
+        total = (
             hit(entry, 0) * pieces[table[entry, 0]] + hit(entry, 1) * pieces[table[entry, 1]]
         )
+        return jnp.where(core == 0, total, turned(total))
 
     def multiply(matrix, row, held, chunks):
         tall = min(held, B)
         totals = []
-        for first in range(0, held, tall):
+        for first in range(row, row + held, tall):
             total = None
             column = 0
             for right in chunks:
                 depth = right.shape[0]
-                left = stack(matrix[row + first : row + first + tall, column : column + depth])
+                left = matrix[2 * first : 2 * (first + tall), column : column + depth]
                 part = dot(left, right)
                 total = part if total is None else total + part
                 column += depth
-            totals.append(fold(total))
+            totals.append(fold_narrow(total))
         return totals[0] if len(totals) == 1 else jnp.concatenate(totals, axis=0)
 
+    def together(pair, before, after):
+        before()
+
+        def start(c):
+            for gather in pair:
+                gather.middle(c)
+
+        both(start)
+        for stream, gather in enumerate(pair):
+
+            def rest(c, gather=gather):
+                gather.close(c)
+                gather.finish(c)
+
+            both(rest)
+            after(stream)
+
+    send_update(0, 0, -acc_v[...])
+    send_update(1, 0, turned(-acc_v[...]))
+
+    def before_first():
+        both(lambda c: [gather.middle(c) for gather in hs])
+        store(y_v, solved_out)
+        fill(1)
+        loads[13].wait()
+        widen(m_v, ms_v, 1, 0, HELD[0])
+        loads[14].wait()
+        widen(e_v, es_v, 1, 0, HELD[0])
+
+    def nothing():
+        pass
+
     piv_row = 0
-    upd_row = 0
     for level in range(1, LEVELS + 1):
         held = HELD[level - 1]
-        value = multiply(m_v, piv_row, held, [side(p_v[...])])
-        if level == LEVELS:
-            last_v[...] = value
-            store(last_v, front_out.at[pl.ds(piv_row, held)])
+        rows = pl.ds(piv_row, held)
+        last = level == LEVELS
+
+        def pivots(stream, level=level, row=piv_row, held=held, last=last):
+            place(stream, level)
+            value = multiply(ms_v, row, held, [narrow(p_v[stream])])
+            if not last:
+                gather = zs[stream][level - 1]
+                own = mine(gather)
+                gather.buf[own] = pack(value)
+                both(gather.begin)
+            if stream == 0:
+                z_v[row : row + held, :] = value
+            else:
+                z_v[row : row + held, :] = merged(z_v[row : row + held, :], value)
+
+        together([ws[0][level - 1], ws[1][level - 1]], before_first if level == 1 else nothing, pivots)
+        store(z_v.at[rows], front_out.at[rows])
+        if last:
             break
-        gather = zs[level - 1]
-        at_own = mine(gather)
-        gather.buf[at_own] = value
-
-        def before_solution(level=level, gather=gather, row=piv_row, held=held):
-            store(gather.buf.at[mine(gather)], front_out.at[pl.ds(row, held)])
+
+        def prepare_next(level=level, row=piv_row, held=held):
             fill(level + 1)
-
-        run(gather, before_solution)
-        chunks = [
-            side(gather.buf[y, z].reshape(8 * held, N))
-            for y in range(YS[level - 1])
-            for z in range(ZS[level - 1])
-        ]
-        below = update_rows(level) - multiply(e_v, upd_row, held, chunks)
-        wide = ws[level]
-        wide_at = mine(wide)
-        wide.buf[wide_at] = below
-        run(wide, lambda: None)
-        place(level + 1)
+            widen(m_v, ms_v, level + 1, row + held, HELD[level])
+            if level + 1 < LEVELS:
+                widen(e_v, es_v, level + 1, row + held, HELD[level])
+
+        def updates(stream, level=level, row=piv_row, held=held):
+            gather = zs[stream][level - 1]
+            chunks = [
+                narrow(unpack(gather.buf[y, z].reshape(4 * held, N), min(held, B)))
+                for y in range(YS[level - 1])
+                for z in range(ZS[level - 1])
+            ]
+            value = update_rows(stream, level) - multiply(es_v, row, held, chunks)
+            send_update(stream, level, value)
+
+        together([zs[0][level - 1], zs[1][level - 1]], prepare_next, updates)
         piv_row += held
-        upd_row += held
 
     both(lambda c: [gather.drain(c) for gather in gathers])
     for copy in stores:
@@ -441,7 +517,8 @@
         place = jnp.sum(match * jnp.arange(PB, dtype=jnp.int32), axis=2, dtype=jnp.int32)
         place = place + jnp.array([0, PB], jnp.int32)
         last = jnp.arange(PB + 1)[:, None] == PB
-        place = jnp.where(last, place * (B // held) + row % B // held, place)
+        unit = min(B, 2 * held)
+        place = jnp.where(last, place * (B // unit) + row % B // unit, place)
         places.append(jnp.pad(place, ((0, 0), (0, 6))))
         flags.append(jnp.pad(match.any(axis=2), ((0, 0), (0, 6))))
     found = jnp.concatenate([jnp.concatenate(places), jnp.concatenate(flags).astype(jnp.int32)], axis=1)
@@ -467,18 +544,22 @@
         pltpu.VMEM((2, 2 * B, 2 * B), BF16),
         pltpu.VMEM((2, B, N), F32),
         pltpu.VMEM((2 * B, N), F32),
-        pltpu.VMEM((ROWS, N), F32),
-        pltpu.VMEM((HELD[-1], N), F32),
+        pltpu.VMEM((2, ROWS, N), F32),
+        pltpu.VMEM((2 * PROWS, ROWS), BF16),
+        pltpu.VMEM((2 * UROWS, ROWS), BF16),
+        pltpu.VMEM((PROWS, N), F32),
     ]
     scratch += [wide(level, HELD[level - 1]) for level in range(1, 6)]
-    scratch += [wide(1, 256)]
-    scratch += [wide(level + 1, HELD[level - 1]) for level in range(1, 5)]
-    scratch += [wide(level, HELD[level - 1]) for level in range(1, 5)]
+    for _ in range(2):
+        scratch += [wide(1, B)]
+        scratch += [wide(level + 1, HELD[level - 1] // 2) for level in range(1, 5)]
+        scratch += [wide(level, HELD[level - 1] // 2) for level in range(1, 5)]
+    copies = sum(COPIES) + 2 * (sum(COPIES) + sum(COPIES[:4]))
     scratch += [
-        pltpu.SemaphoreType.DMA((11,)),
+        pltpu.SemaphoreType.DMA((15,)),
         pltpu.SemaphoreType.DMA((6,)),
-        pltpu.SemaphoreType.DMA((14, COPIES)),
-        pltpu.SemaphoreType.DMA((14, COPIES)),
+        pltpu.SemaphoreType.DMA((copies,)),
+        pltpu.SemaphoreType.DMA((copies,)),
     ]
     smem = pl.BlockSpec(memory_space=pltpu.SMEM)
     hbm = pl.BlockSpec(memory_space=pl.ANY)

time: 155 us -> 145 us (0.935)
  Pallas kernels: 147 us -> 136 us
    pallas_call x1, Pallas kernels: 147 us -> 136 us  [per_device(): pl.pallas_call(kernel, out_shape=(jax.ShapeDtypeStruct((SB, B, N), F32),...]
where the time goes in v4:
time: 145 us; the launch traced here: 144 us
  Pallas kernels  136 us (94%)
  local copies, waits for them, and re-layouts  6.35 us (4%)
    pallas_call x1, Pallas kernels, per_device(): pl.pallas_call(kernel, out_shape=(jax.ShapeDtypeStruct((SB, B, N), F32),...  136 us
    unnamed x6, local copies, waits for them, and re-layouts  3.4 us

profile of v4, /device:TPU:1, one launch (start us, length us, event | category | flops | bytes accessed | tf_op | source)
XLA Modules:
  0.0 144.4 jit_solution(18187107552754372063)
XLA Ops:
  0.6 0.0 copy-start
  1.0 0.7 slice.7
  1.6 0.1 constant_dynamic-slice_fusion.4
  1.7 0.1 pad_add_fusion.5
  1.8 0.1 pad_add_fusion.1
  1.9 0.1 broadcast_compare_fusion
  2.0 0.1 bitcast_add_fusion
  2.0 0.9 constant_dynamic-slice_fusion
  3.0 0.1 copy.29
  3.0 0.1 copy.27
  3.1 0.1 copy.26
  3.2 0.1 copy.28
  3.3 0.1 compare_reduce_fusion
  3.4 0.1 fusion.2
  3.5 0.1 compare_reduce_fusion.2
  3.6 0.1 fusion
  3.7 0.1 add_select_fusion.2
  3.8 0.1 concatenate.33
  3.9 0.1 concatenate.32
  4.0 0.1 pad_add_fusion
  4.1 0.7 copy.30.table
  4.8 136.2 %shard_map.149 = (f32[24,128,128]{2,1,0:T(8,128)}, f32[496,128]{1,0:T(8,128)}) custom-call(s32[109,16]{1,0:T(8,128)} %copy.30.table, f32[24,128,128]{2,1,0:T(8,128)} %bitcast.8, f32[24,128,128]{2,1,0:T(8,128)} %dinv.1, f32[23,2,128,128]{3,2,1,0:T(8,128)} %off.1, f32[256,3072]{1,0:T(8,128)} %update.1, f32[496,128]{1,0:T(8,128)} %front_rhs.1, ...), custom_call_target="tpu_custom_call" | custom-call | tf_op jit(solution)/shard_map/pallas_call | solution.py:566
  141.0 2.7 %copy.33 = f32[3072,128]{1,0:T(8,128)} copy(f32[3072,128]{1,0:T(8,128)} %bitcast.9) | data formatting | bytes 3145728
  143.7 0.7 copy.34
  (18 shorter events, 0.1 us)
Async XLA Ops:
  0.6 1.0 copy-start
  141.0 2.7 %copy-start.1 = (f32[496,128]{1,0:T(8,128)S(1)}, f32[496,128]{1,0:T(8,128)}, u32[]{:S(2)}) copy-start(f32[496,128]{1,0:T(8,128)} %get-tuple-element.31) | copy-start | bytes 761860

commit v5 on v4

--- a/solution.py
+++ b/solution.py
@@ -63,36 +63,38 @@
     return pltpu.roll(value, HALF, 1)
 
 
-def merged(left, right):
-    return jnp.where(low_half(left.shape), left, turned(right))
-
-
-def pack(value):
-    rows = value.shape[0]
-    unit = min(rows, B)
-    parts = []
-    for first in range(0, rows, unit):
-        middle = first + unit // 2
-        parts.append(merged(value[first:middle], value[middle : first + unit]))
-    return parts[0] if len(parts) == 1 else jnp.concatenate(parts, axis=0)
-
-
-def unpack(value, unit):
-    rows = value.shape[0]
-    shape = (2 * rows // unit, unit // 2, N)
-    pair = jnp.concatenate([value.reshape(shape), turned(value).reshape(shape)], axis=1)
-    return pair.reshape(2 * rows, N)
-
-
-def narrow(value):
-    high = value.astype(BF16).astype(F32)
-    return merged(high, value - high).astype(BF16)
-
-
-def fold_narrow(product):
+def choose(low, high):
+    return jnp.where(low_half(low.shape), low, high)
+
+
+def pairs(value, unit):
+    many = value.shape[0]
+    blocks = value.reshape(many // unit, unit, N)
+    shape = (many // 2, N)
+    return blocks[:, : unit // 2].reshape(shape), blocks[:, unit // 2 :].reshape(shape)
+
+
+def streams_of(value, unit):
+    lower, upper = pairs(value, unit)
+    return choose(lower, turned(upper)), choose(turned(lower), upper)
+
+
+def pack(value, unit):
+    return choose(*pairs(value, unit))
+
+
+def operand(packed, unit):
+    high = packed.astype(BF16).astype(F32)
+    low = turned(packed - high)
+    shape = (2 * packed.shape[0] // unit, unit // 2, N)
+    pair = [choose(high, low).reshape(shape), choose(low, high).reshape(shape)]
+    return jnp.concatenate(pair, axis=1).reshape(2 * packed.shape[0], N).astype(BF16)
+
+
+def fold_both(product):
     half = product.shape[0] // 2
-    top = product[:half]
-    return top + (turned(top) + product[half:])
+    total = product[:half] + product[half:]
+    return total + turned(total)
 
 
 class Gather:
@@ -223,7 +225,7 @@
     table,
     rhs, dinv, off, update, front_rhs, piv, factor,
     solved_out, front_out,
-    b_v, d_v, l_v, u_v, m_v, e_v, y_v, yhl_v, g_v, c_v, acc_v, p_v, ms_v, es_v, z_v,
+    b_v, d_v, l_v, u_v, m_v, e_v, y_v, yhl_v, g_v, c_v, acc_v, p_v, rhs_v, ms_v, es_v, z_v,
     h1, h2, h3, h4, h5, *rest,
 ):
     leaf = lax.axis_index("leaf")
@@ -337,10 +339,13 @@
         copy.start()
         stores.append(copy)
 
-    def widen(source, target, level, row, held):
+    def widen(source, target, row, held):
         tall = min(held, B)
         for first in range(row, row + held, tall):
             target[2 * first : 2 * (first + tall), :] = stack(source[first : first + tall, :])
+
+    def unit_of(level):
+        return B if level == 1 else min(B, HELD[level - 2])
 
     def fill(level):
         gather = hs[level - 1]
@@ -355,14 +360,14 @@
         for y in range(YS[level - 1]):
             for z in range(ZS[level - 1]):
                 first = (y * ZS[level - 1] + z) * many
-                part = gather.buf[y, z].reshape(many, N)
-                p_v[0, first : first + many, :] = part
-                p_v[1, first : first + many, :] = turned(part)
+                rows = slice(first // 2, (first + many) // 2)
+                parts = streams_of(gather.buf[y, z].reshape(many, N), unit_of(level))
+                p_v[0, rows, :], p_v[1, rows, :] = parts
 
     def send_update(stream, level, value):
         gather = ws[stream][level]
         own = mine(gather)
-        gather.buf[own] = pack(value)
+        gather.buf[own] = value
         both(gather.begin)
 
     def hit(entry, which):
@@ -377,29 +382,28 @@
         return total
 
     def place(stream, level):
-        unit = B if level == 1 else min(B, HELD[level - 2])
-
         def body(block, carry):
+            packed = pl.ds(pl.multiple_of(block * HALF, HALF), HALF)
             rows = pl.ds(pl.multiple_of(block * B, B), B)
-            total = unpack(landed(stream, level, ENTRY_AT[level] + block), unit)
-            p_v[stream, rows, :] = p_v[stream, rows, :] + total
+            total = p_v[stream, packed, :] + landed(stream, level, ENTRY_AT[level] + block)
+            rhs_v[rows, :] = operand(total, unit_of(level))
             return carry
 
-        lax.fori_loop(0, PB, body, 0)
+        lax.fori_loop(0, PB, body, 0, unroll=4)
 
     def update_rows(stream, level):
         entry = ENTRY_AT[level] + PB
         if level == 1:
-            parts = [unpack(landed(stream, 1, entry + i), B) for i in (0, 1)]
-            return jnp.concatenate(parts, axis=0)
+            return jnp.concatenate([landed(stream, 1, entry + i) for i in (0, 1)], axis=0)
         if level == 2:
-            return unpack(landed(stream, 2, entry), B)
+            return landed(stream, 2, entry)
         held = HELD[level - 1]
         pieces = ws[stream][level - 1].buf.reshape(ROWS // held, held, N)
         total = (
             hit(entry, 0) * pieces[table[entry, 0]] + hit(entry, 1) * pieces[table[entry, 1]]
         )
-        return jnp.where(core == 0, total, turned(total))
+        lower, upper = pairs(jnp.where(core == 0, total, turned(total)), held)
+        return choose(lower, turned(upper))
 
     def multiply(matrix, row, held, chunks):
         tall = min(held, B)
@@ -413,7 +417,7 @@
                 part = dot(left, right)
                 total = part if total is None else total + part
                 column += depth
-            totals.append(fold_narrow(total))
+            totals.append(fold_both(total))
         return totals[0] if len(totals) == 1 else jnp.concatenate(totals, axis=0)
 
     def together(pair, before, after):
@@ -433,17 +437,17 @@
             both(rest)
             after(stream)
 
-    send_update(0, 0, -acc_v[...])
-    send_update(1, 0, turned(-acc_v[...]))
+    for stream, value in enumerate(streams_of(-acc_v[...], B)):
+        send_update(stream, 0, value)
 
     def before_first():
         both(lambda c: [gather.middle(c) for gather in hs])
         store(y_v, solved_out)
         fill(1)
         loads[13].wait()
-        widen(m_v, ms_v, 1, 0, HELD[0])
+        widen(m_v, ms_v, 0, HELD[0])
         loads[14].wait()
-        widen(e_v, es_v, 1, 0, HELD[0])
+        widen(e_v, es_v, 0, HELD[0])
 
     def nothing():
         pass
@@ -456,16 +460,16 @@
 
         def pivots(stream, level=level, row=piv_row, held=held, last=last):
             place(stream, level)
-            value = multiply(ms_v, row, held, [narrow(p_v[stream])])
+            value = multiply(ms_v, row, held, [rhs_v[...]])
             if not last:
                 gather = zs[stream][level - 1]
                 own = mine(gather)
-                gather.buf[own] = pack(value)
+                gather.buf[own] = pack(value, min(held, B))
                 both(gather.begin)
             if stream == 0:
                 z_v[row : row + held, :] = value
             else:
-                z_v[row : row + held, :] = merged(z_v[row : row + held, :], value)
+                z_v[row : row + held, :] = choose(z_v[row : row + held, :], value)
 
         together([ws[0][level - 1], ws[1][level - 1]], before_first if level == 1 else nothing, pivots)
         store(z_v.at[rows], front_out.at[rows])
@@ -474,19 +478,19 @@
 
         def prepare_next(level=level, row=piv_row, held=held):
             fill(level + 1)
-            widen(m_v, ms_v, level + 1, row + held, HELD[level])
+            widen(m_v, ms_v, row + held, HELD[level])
             if level + 1 < LEVELS:
-                widen(e_v, es_v, level + 1, row + held, HELD[level])
+                widen(e_v, es_v, row + held, HELD[level])
 
         def updates(stream, level=level, row=piv_row, held=held):
             gather = zs[stream][level - 1]
             chunks = [
-                narrow(unpack(gather.buf[y, z].reshape(4 * held, N), min(held, B)))
+                operand(gather.buf[y, z].reshape(4 * held, N), min(held, B))
                 for y in range(YS[level - 1])
                 for z in range(ZS[level - 1])
             ]
-            value = update_rows(stream, level) - multiply(es_v, row, held, chunks)
-            send_update(stream, level, value)
+            value = pack(multiply(es_v, row, held, chunks), min(held, B))
+            send_update(stream, level, update_rows(stream, level) - value)
 
         together([zs[0][level - 1], zs[1][level - 1]], prepare_next, updates)
         piv_row += held
@@ -544,7 +548,8 @@
         pltpu.VMEM((2, 2 * B, 2 * B), BF16),
         pltpu.VMEM((2, B, N), F32),
         pltpu.VMEM((2 * B, N), F32),
-        pltpu.VMEM((2, ROWS, N), F32),
+        pltpu.VMEM((2, ROWS // 2, N), F32),
+        pltpu.VMEM((ROWS, N), BF16),
         pltpu.VMEM((2 * PROWS, ROWS), BF16),
         pltpu.VMEM((2 * UROWS, ROWS), BF16),
         pltpu.VMEM((PROWS, N), F32),

time: 145 us -> 136 us (0.938)
  Pallas kernels: 136 us -> 128 us
    pallas_call x1, Pallas kernels: 136 us -> 128 us  [per_device(): pl.pallas_call(kernel, out_shape=(jax.ShapeDtypeStruct((SB, B, N), F32),...]
where the time goes in v5:
time: 136 us
  Pallas kernels  128 us (94%)
  local copies, waits for them, and re-layouts  6.35 us (5%)
    pallas_call x1, Pallas kernels, per_device(): pl.pallas_call(kernel, out_shape=(jax.ShapeDtypeStruct((SB, B, N), F32),...  128 us
    unnamed x6, local copies, waits for them, and re-layouts  3.4 us

profile of v5, /device:TPU:1, one launch (start us, length us, event | category | flops | bytes accessed | tf_op | source)
XLA Modules:
  0.0 135.9 jit_solution(5655230760512745996)
XLA Ops:
  0.6 0.0 copy-start
  1.0 0.7 slice.7
  1.6 0.1 constant_dynamic-slice_fusion.4
  1.7 0.1 pad_add_fusion.5
  1.8 0.1 pad_add_fusion.1
  1.9 0.1 broadcast_compare_fusion
  2.0 0.1 bitcast_add_fusion
  2.0 0.9 constant_dynamic-slice_fusion
  3.0 0.1 copy.29
  3.0 0.1 copy.27
  3.1 0.1 copy.26
  3.2 0.1 copy.28
  3.3 0.1 compare_reduce_fusion
  3.4 0.1 fusion.2
  3.5 0.1 compare_reduce_fusion.2
  3.6 0.1 fusion
  3.7 0.1 add_select_fusion.2
  3.8 0.1 concatenate.33
  3.9 0.1 concatenate.32
  4.0 0.1 pad_add_fusion
  4.1 0.7 copy.30.table
  4.8 127.7 %shard_map.149 = (f32[24,128,128]{2,1,0:T(8,128)}, f32[496,128]{1,0:T(8,128)}) custom-call(s32[109,16]{1,0:T(8,128)} %copy.30.table, f32[24,128,128]{2,1,0:T(8,128)} %bitcast.8, f32[24,128,128]{2,1,0:T(8,128)} %dinv.1, f32[23,2,128,128]{3,2,1,0:T(8,128)} %off.1, f32[256,3072]{1,0:T(8,128)} %update.1, f32[496,128]{1,0:T(8,128)} %front_rhs.1, ...), custom_call_target="tpu_custom_call" | custom-call | tf_op jit(solution)/shard_map/pallas_call | solution.py:571
  132.6 2.7 %copy.33 = f32[3072,128]{1,0:T(8,128)} copy(f32[3072,128]{1,0:T(8,128)} %bitcast.9) | data formatting | bytes 3145728
  135.2 0.7 copy.34
  (18 shorter events, 0.1 us)
Async XLA Ops:
  0.6 1.0 copy-start
  132.5 2.7 %copy-start.1 = (f32[496,128]{1,0:T(8,128)S(1)}, f32[496,128]{1,0:T(8,128)}, u32[]{:S(2)}) copy-start(f32[496,128]{1,0:T(8,128)} %get-tuple-element.31) | copy-start | bytes 761860

commit v6 on v5

--- a/solution.py
+++ b/solution.py
@@ -25,7 +25,6 @@
 MIXED = (("x", "zy"), ("zy", "x"))
 SAME = (("x", "zy"), ("x", "zy"))
 SENDS = (3, 7, 15, 10, 18)
-COPIES = (7, 12, 22, 21, 37)
 HALF = 64
 COLUMNS_AT = 86
 EARLY = 8
@@ -98,9 +97,9 @@
 
 
 class Gather:
-    def __init__(self, buf, send, recv, base, level, at, order):
+    def __init__(self, buf, send, recv, level, at, order):
         self.buf, self.send, self.recv, self.at = buf, send, recv, at
-        self.base, self.level, eager = base, level, level < 4
+        self.level, eager = level, level < 4
         self.size = {"x": 4, "z": ZS[level - 1], "y": YS[level - 1]}
         self.order, self.eager = order, eager
         self.own = {d: 0 if self.size[d] == 1 else at[d] % self.size[d] for d in "yzx"}
@@ -140,8 +139,8 @@
         return pltpu.make_async_remote_copy(
             src_ref=view,
             dst_ref=view,
-            send_sem=self.send.at[self.base + which],
-            recv_sem=self.recv.at[self.base + which],
+            send_sem=self.send,
+            recv_sem=self.recv.at[which],
             device_id=(place["y"] * 4 + place["z"], place["x"] * 2 + place["core"]),
             device_id_type=pl.DeviceIdType.MESH,
         )
@@ -161,7 +160,6 @@
         cross = SENDS[self.level - 1]
         begin = [self.out(self.view(core), i, core, step) for i, step in enumerate(near)]
         used = len(near)
-        mine = [(self.view(core), cross)]
         middle, close = [], []
         held = [{}] + [self.origin(step) for step in near]
         sets = [held[i : i + 1] for i in range(len(held))] if self.eager else [held]
@@ -174,9 +172,8 @@
             begin += sends[0]
         for i, step in enumerate(near):
             view = self.view(core, **held[i + 1])
-            mine.append((view, cross + 1 + i))
             after = sends[i + 1] if self.eager else sends[0] if i == len(near) - 1 else []
-            middle.append(([(view, i)], after + [self.across(view, cross + 1 + i, core)]))
+            middle.append(([(view, i)], after + [self.across(view, cross, core)]))
         if not second:
             middle = [(wait, [start[-1]]) for wait, start in middle]
         for j, step in enumerate(far):
@@ -188,11 +185,10 @@
                 else:
                     view = self.view(core, first, **origin)
                 waits.append((view, len(near) + g * len(far) + j))
-            view, which = self.view(core, first, **origin), cross + 1 + len(near) + j
-            mine.append((view, which))
-            close.append((waits, [self.across(view, which, core)]))
+            view = self.view(core, first, **origin)
+            close.append((waits, [self.across(view, cross, core)]))
         begin.append(self.across(self.view(core), cross, core))
-        return begin, middle, close, mine
+        return begin, middle, close
 
     def begin(self, core):
         for make in self.plan(core)[0]:
@@ -212,13 +208,13 @@
         self.follow(self.plan(core)[2], core)
 
     def finish(self, core):
-        for view, which in self.plan(1 - core)[3]:
-            self.copy(view, which, core=1 - core).wait_recv()
-
-    def drain(self, core):
-        begin, middle, close, _ = self.plan(core)
-        for make in begin + [make for _, starts in middle + close for make in starts]:
-            make().wait_send()
+        half = self.view(1 - core, "yzx")
+        self.copy(half, SENDS[self.level - 1], core=1 - core).wait_recv()
+
+    def drain(self, spare):
+        rows = (8 * self.size["y"] * self.size["z"] - 1) * self.buf.shape[-2]
+        view = spare.at[pl.ds(0, rows)]
+        self.copy(view, 0, core=1 - self.at["core"]).wait_send()
 
 
 def kernel(
@@ -245,8 +241,11 @@
     base = 0
     for buf, level in zip((h1, h2, h3, h4, h5, *streams), levels):
         order = SAME if len(gathers) < 5 else MIXED
-        gathers.append(Gather(buf, send, recv, base, level, at, order))
-        base += COPIES[level - 1]
+        copies = SENDS[level - 1] + 1
+        gathers.append(
+            Gather(buf, send.at[len(gathers)], recv.at[pl.ds(base, copies)], level, at, order)
+        )
+        base += copies
     hs = gathers[:5]
     ws = (gathers[5:10], gathers[14:19])
     zs = (gathers[10:14], gathers[19:23])
@@ -495,7 +494,9 @@
         together([zs[0][level - 1], zs[1][level - 1]], prepare_next, updates)
         piv_row += held
 
-    both(lambda c: [gather.drain(c) for gather in gathers])
+    spare = b_v.reshape(SB * B, N)
+    for gather in gathers:
+        gather.drain(spare)
     for copy in stores:
         copy.wait()
 
@@ -559,11 +560,11 @@
         scratch += [wide(1, B)]
         scratch += [wide(level + 1, HELD[level - 1] // 2) for level in range(1, 5)]
         scratch += [wide(level, HELD[level - 1] // 2) for level in range(1, 5)]
-    copies = sum(COPIES) + 2 * (sum(COPIES) + sum(COPIES[:4]))
+    copies = 3 * sum(SENDS) + 2 * sum(SENDS[:4]) + 23
     scratch += [
         pltpu.SemaphoreType.DMA((15,)),
         pltpu.SemaphoreType.DMA((6,)),
-        pltpu.SemaphoreType.DMA((copies,)),
+        pltpu.SemaphoreType.DMA((23,)),
         pltpu.SemaphoreType.DMA((copies,)),
     ]
     smem = pl.BlockSpec(memory_space=pltpu.SMEM)

time: 136 us -> 131 us (0.963)
  Pallas kernels: 128 us -> 123 us
    pallas_call x1, Pallas kernels: 128 us -> 123 us  [per_device(): pl.pallas_call(kernel, out_shape=(jax.ShapeDtypeStruct((SB, B, N), F32),...]
where the time goes in v6:
time: 131 us
  Pallas kernels  123 us (94%)
  local copies, waits for them, and re-layouts  6.35 us (5%)
    pallas_call x1, Pallas kernels, per_device(): pl.pallas_call(kernel, out_shape=(jax.ShapeDtypeStruct((SB, B, N), F32),...  123 us
    unnamed x6, local copies, waits for them, and re-layouts  3.4 us

profile of v6, /device:TPU:1, one launch (start us, length us, event | category | flops | bytes accessed | tf_op | source)
XLA Modules:
  0.0 130.8 jit_solution(1719961428819807610)
XLA Ops:
  0.6 0.0 copy-start
  1.0 0.7 slice.7
  1.6 0.1 constant_dynamic-slice_fusion.4
  1.7 0.1 pad_add_fusion.5
  1.8 0.1 pad_add_fusion.1
  1.9 0.1 broadcast_compare_fusion
  2.0 0.1 bitcast_add_fusion
  2.0 0.9 constant_dynamic-slice_fusion
  3.0 0.1 copy.29
  3.0 0.1 copy.27
  3.1 0.1 copy.26
  3.2 0.1 copy.28
  3.3 0.1 compare_reduce_fusion
  3.4 0.1 fusion.2
  3.5 0.1 compare_reduce_fusion.2
  3.6 0.1 fusion
  3.7 0.1 add_select_fusion.2
  3.8 0.1 concatenate.33
  3.9 0.1 concatenate.32
  4.0 0.1 pad_add_fusion
  4.1 0.7 copy.30.table
  4.8 122.6 %shard_map.149 = (f32[24,128,128]{2,1,0:T(8,128)}, f32[496,128]{1,0:T(8,128)}) custom-call(s32[109,16]{1,0:T(8,128)} %copy.30.table, f32[24,128,128]{2,1,0:T(8,128)} %bitcast.8, f32[24,128,128]{2,1,0:T(8,128)} %dinv.1, f32[23,2,128,128]{3,2,1,0:T(8,128)} %off.1, f32[256,3072]{1,0:T(8,128)} %update.1, f32[496,128]{1,0:T(8,128)} %front_rhs.1, ...), custom_call_target="tpu_custom_call" | custom-call | tf_op jit(solution)/shard_map/pallas_call | solution.py:572
  127.4 2.7 %copy.33 = f32[3072,128]{1,0:T(8,128)} copy(f32[3072,128]{1,0:T(8,128)} %bitcast.9) | data formatting | bytes 3145728
  130.1 0.7 copy.34
  (18 shorter events, 0.1 us)
Async XLA Ops:
  0.6 1.0 copy-start
  127.4 2.7 %copy-start.1 = (f32[496,128]{1,0:T(8,128)S(1)}, f32[496,128]{1,0:T(8,128)}, u32[]{:S(2)}) copy-start(f32[496,128]{1,0:T(8,128)} %get-tuple-element.31) | copy-start | bytes 761860

commit v7 on v6

--- a/solution.py
+++ b/solution.py
@@ -349,11 +349,7 @@
     def fill(level):
         gather = hs[level - 1]
 
-        def rest(c):
-            gather.close(c)
-            gather.finish(c)
-
-        both(rest)
+        both(gather.finish)
         held = HELD[level - 1]
         many = 8 * held
         for y in range(YS[level - 1]):
@@ -388,7 +384,7 @@
             rhs_v[rows, :] = operand(total, unit_of(level))
             return carry
 
-        lax.fori_loop(0, PB, body, 0, unroll=4)
+        lax.fori_loop(0, PB, body, 0, unroll=8)
 
     def update_rows(stream, level):
         entry = ENTRY_AT[level] + PB
@@ -448,14 +444,15 @@
         loads[14].wait()
         widen(e_v, es_v, 0, HELD[0])
 
-    def nothing():
-        pass
-
     piv_row = 0
     for level in range(1, LEVELS + 1):
         held = HELD[level - 1]
         rows = pl.ds(piv_row, held)
         last = level == LEVELS
+
+        def before_pivots(level=level):
+            if level < LEVELS:
+                both(hs[level].close)
 
         def pivots(stream, level=level, row=piv_row, held=held, last=last):
             place(stream, level)
@@ -465,21 +462,23 @@
                 own = mine(gather)
                 gather.buf[own] = pack(value, min(held, B))
                 both(gather.begin)
+            if level == 1 and stream == 0:
+                both(hs[1].close)
             if stream == 0:
                 z_v[row : row + held, :] = value
             else:
                 z_v[row : row + held, :] = choose(z_v[row : row + held, :], value)
 
-        together([ws[0][level - 1], ws[1][level - 1]], before_first if level == 1 else nothing, pivots)
+        together([ws[0][level - 1], ws[1][level - 1]], before_first if level == 1 else before_pivots, pivots)
         store(z_v.at[rows], front_out.at[rows])
         if last:
             break
 
         def prepare_next(level=level, row=piv_row, held=held):
-            fill(level + 1)
             widen(m_v, ms_v, row + held, HELD[level])
             if level + 1 < LEVELS:
                 widen(e_v, es_v, row + held, HELD[level])
+            fill(level + 1)
 
         def updates(stream, level=level, row=piv_row, held=held):
             gather = zs[stream][level - 1]

time: 131 us -> 129 us (0.985)
  Pallas kernels: 123 us -> 120 us
    pallas_call x1, Pallas kernels: 123 us -> 120 us  [per_device(): pl.pallas_call(kernel, out_shape=(jax.ShapeDtypeStruct((SB, B, N), F32),...]
where the time goes in v7:
time: 129 us; the launch traced here: 128 us
  Pallas kernels  120 us (93%)
  local copies, waits for them, and re-layouts  6.35 us (5%)
    pallas_call x1, Pallas kernels, per_device(): pl.pallas_call(kernel, out_shape=(jax.ShapeDtypeStruct((SB, B, N), F32),...  120 us
    unnamed x6, local copies, waits for them, and re-layouts  3.4 us

profile of v7, /device:TPU:1, one launch (start us, length us, event | category | flops | bytes accessed | tf_op | source)
XLA Modules:
  0.0 128.4 jit_solution(17663402759834121589)
XLA Ops:
  0.6 0.0 copy-start
  1.0 0.7 slice.7
  1.6 0.1 constant_dynamic-slice_fusion.4
  1.7 0.1 pad_add_fusion.5
  1.8 0.1 pad_add_fusion.1
  1.9 0.1 broadcast_compare_fusion
  2.0 0.1 bitcast_add_fusion
  2.0 0.9 constant_dynamic-slice_fusion
  3.0 0.1 copy.29
  3.0 0.1 copy.27
  3.1 0.1 copy.26
  3.2 0.1 copy.28
  3.3 0.1 compare_reduce_fusion
  3.4 0.1 fusion.2
  3.5 0.1 compare_reduce_fusion.2
  3.6 0.1 fusion
  3.7 0.1 add_select_fusion.2
  3.8 0.1 concatenate.33
  3.9 0.1 concatenate.32
  4.0 0.1 pad_add_fusion
  4.1 0.7 copy.30.table
  4.8 120.2 %shard_map.149 = (f32[24,128,128]{2,1,0:T(8,128)}, f32[496,128]{1,0:T(8,128)}) custom-call(s32[109,16]{1,0:T(8,128)} %copy.30.table, f32[24,128,128]{2,1,0:T(8,128)} %bitcast.8, f32[24,128,128]{2,1,0:T(8,128)} %dinv.1, f32[23,2,128,128]{3,2,1,0:T(8,128)} %off.1, f32[256,3072]{1,0:T(8,128)} %update.1, f32[496,128]{1,0:T(8,128)} %front_rhs.1, ...), custom_call_target="tpu_custom_call" | custom-call | tf_op jit(solution)/shard_map/pallas_call | solution.py:571
  125.0 2.7 %copy.33 = f32[3072,128]{1,0:T(8,128)} copy(f32[3072,128]{1,0:T(8,128)} %bitcast.9) | data formatting | bytes 3145728
  127.7 0.7 copy.34
  (18 shorter events, 0.1 us)
Async XLA Ops:
  0.6 1.0 copy-start
  125.0 2.7 %copy-start.1 = (f32[496,128]{1,0:T(8,128)S(1)}, f32[496,128]{1,0:T(8,128)}, u32[]{:S(2)}) copy-start(f32[496,128]{1,0:T(8,128)} %get-tuple-element.31) | copy-start | bytes 761860

commit v8 on v7

--- a/solution.py
+++ b/solution.py
@@ -27,7 +27,7 @@
 SENDS = (3, 7, 15, 10, 18)
 HALF = 64
 COLUMNS_AT = 86
-EARLY = 8
+EARLY = 9
 F32 = jnp.float32
 BF16 = jnp.bfloat16
 
@@ -328,7 +328,7 @@
     lax.fori_loop(1, EARLY - 1, advance, 0)
     for copy in loads[9:13]:
         copy.wait()
-    lax.fori_loop(EARLY - 1, SB, advance, 0)
+    lax.fori_loop(EARLY - 1, SB, advance, 0, unroll=2)
     couple(SB - 1)
 
     stores = []

time: 129 us -> 129 us (level)
  no operation moved by 1% of the time
where the time goes in v8:
time: 129 us
  Pallas kernels  120 us (93%)
  local copies, waits for them, and re-layouts  6.35 us (5%)
    pallas_call x1, Pallas kernels, per_device(): pl.pallas_call(kernel, out_shape=(jax.ShapeDtypeStruct((SB, B, N), F32),...  120 us
    unnamed x6, local copies, waits for them, and re-layouts  3.4 us

profile of v8, /device:TPU:1, one launch (start us, length us, event | category | flops | bytes accessed | tf_op | source)
XLA Modules:
  0.0 128.7 jit_solution(1096492248189768747)
XLA Ops:
  0.6 0.0 copy-start
  1.0 0.7 slice.7
  1.6 0.1 constant_dynamic-slice_fusion.4
  1.7 0.1 pad_add_fusion.5
  1.8 0.1 pad_add_fusion.1
  1.9 0.1 broadcast_compare_fusion
  2.0 0.1 bitcast_add_fusion
  2.0 0.9 constant_dynamic-slice_fusion
  3.0 0.1 copy.29
  3.0 0.1 copy.27
  3.1 0.1 copy.26
  3.2 0.1 copy.28
  3.3 0.1 compare_reduce_fusion
  3.4 0.1 fusion.2
  3.5 0.1 compare_reduce_fusion.2
  3.6 0.1 fusion
  3.7 0.1 add_select_fusion.2
  3.8 0.1 concatenate.33
  3.9 0.1 concatenate.32
  4.0 0.1 pad_add_fusion
  4.1 0.7 copy.30.table
  4.8 120.4 %shard_map.149 = (f32[24,128,128]{2,1,0:T(8,128)}, f32[496,128]{1,0:T(8,128)}) custom-call(s32[109,16]{1,0:T(8,128)} %copy.30.table, f32[24,128,128]{2,1,0:T(8,128)} %bitcast.8, f32[24,128,128]{2,1,0:T(8,128)} %dinv.1, f32[23,2,128,128]{3,2,1,0:T(8,128)} %off.1, f32[256,3072]{1,0:T(8,128)} %update.1, f32[496,128]{1,0:T(8,128)} %front_rhs.1, ...), custom_call_target="tpu_custom_call" | custom-call | tf_op jit(solution)/shard_map/pallas_call | solution.py:571
  125.3 2.7 %copy.33 = f32[3072,128]{1,0:T(8,128)} copy(f32[3072,128]{1,0:T(8,128)} %bitcast.9) | data formatting | bytes 3145728
  128.0 0.7 copy.34
  (18 shorter events, 0.1 us)
Async XLA Ops:
  0.6 1.0 copy-start
  125.3 2.7 %copy-start.1 = (f32[496,128]{1,0:T(8,128)S(1)}, f32[496,128]{1,0:T(8,128)}, u32[]{:S(2)}) copy-start(f32[496,128]{1,0:T(8,128)} %get-tuple-element.31) | copy-start | bytes 761860
